TPU v7x, 32 devices: a whole 2x2x4 slice. The times are simulated.
32 devices in a mesh: lat: 4 (over z), lon: 8 (over y, x, core).
Axes of the slice: x: 2, y: 2, z: 4, core: 2. Of those that a mesh axis runs over, the one named last changes fastest.
Arguments:
- tokens: bfloat16 [48, 192, 512], P('lat', 'lon'), may hold values from -100 to 100
- fine_gain: float32 [512], replicated, may hold values from 0.5 to 1.5
- fine_qkv: bfloat16 [512, 768], replicated, may hold values from -20 to 20
- fine_proj: bfloat16 [256, 512], replicated, may hold values from -0.375 to 0.375
- merge_gain: float32 [2048], replicated, may hold values from 0.5 to 1.5
- merge_weight: bfloat16 [2048, 512], replicated, may hold values from -0.125 to 0.125
- coarse_gain: float32 [512], replicated, may hold values from 0.5 to 1.5
- coarse_qkv: bfloat16 [512, 1536], replicated, may hold values from -20 to 20
- coarse_proj: bfloat16 [512, 512], replicated, may hold values from -0.25 to 0.25
- cotangent: bfloat16 [24, 96, 512], P('lat', 'lon'), may hold values from -6 to 6
Outputs:
- output: bfloat16 [24, 96, 512], P('lat', 'lon')
- grad_tokens: bfloat16 [48, 192, 512], P('lat', 'lon')
- grad_fine_gain: float32 [512], P(('lat', 'lon'))
- grad_fine_qkv: float32 [512, 768], P(('lat', 'lon'))
- grad_fine_proj: float32 [256, 512], P(('lat', 'lon'))
- grad_merge_gain: float32 [2048], P(('lat', 'lon'))
- grad_merge_weight: float32 [2048, 512], P(('lat', 'lon'))
- grad_coarse_gain: float32 [512], P(('lat', 'lon'))
- grad_coarse_qkv: float32 [512, 1536], P(('lat', 'lon'))
- grad_coarse_proj: float32 [512, 512], P(('lat', 'lon'))
All inputs are finite; a program needn't handle non-finite values.
Results may differ from a plain program's by a relative error of at most 0.028.
Values may be sent and summed in bfloat16 or wider, within the bound.
A program may use at most 128 MiB of HBM per device.

v0:
```python
import jax
import jax.numpy as jnp
from jax import lax
from jax.sharding import PartitionSpec as P

HF = 4
HC = 8
WLAT = 6
WLON = 12
SLAT = 3
SLON = 6


EPSILON = 1e-05


def from_behind(value, axis, steps):
    count = lax.axis_size(axis)
    pairs = [(source, (source + steps) % count) for source in range(count)]
    return lax.ppermute(value, axis, pairs)


def layer_norm(values, gains):
    center = jnp.mean(values, axis=-1, keepdims=True)
    shifted = values - center
    spread = jnp.mean(shifted * shifted, axis=-1, keepdims=True)
    return shifted * lax.rsqrt(spread + EPSILON) * gains


def window_attention(packed, row_offset, total_rows, head_count):
    row_count, col_count = (packed.shape[0], packed.shape[1])
    head_size = packed.shape[2] // (3 * head_count)
    lat_windows = row_count // WLAT
    lon_windows = col_count // WLON
    grouped = packed.reshape(lat_windows, WLAT, lon_windows, WLON, 3, head_count, head_size)
    grouped = grouped.transpose(4, 0, 2, 5, 1, 3, 6).reshape(
        3, lat_windows, lon_windows, head_count, WLAT * WLON, head_size
    )
    queries = grouped[0].astype(jnp.float32)
    keys_all = grouped[1].astype(jnp.float32)
    values_all = grouped[2].astype(jnp.float32)
    scores = jnp.einsum("abhqd,abhkd->abhqk", queries, keys_all) * head_size ** (-0.5)
    row_index = row_offset + jnp.arange(row_count, dtype=jnp.int32)
    region = (row_index >= total_rows - SLAT).reshape(lat_windows, WLAT)
    region = jnp.broadcast_to(region[:, :, None], (lat_windows, WLAT, WLON)).reshape(
        lat_windows, WLAT * WLON
    )
    allowed = region[:, None, None, :, None] == region[:, None, None, None, :]
    scores = jnp.where(allowed, scores, -1000000000.0)
    largest = jnp.max(scores, axis=-1, keepdims=True)
    exponent = jnp.exp(scores - largest)
    attn_weights = (exponent / jnp.sum(exponent, axis=-1, keepdims=True)).astype(jnp.bfloat16)
    mixed_out = jnp.einsum(
        "abhqk,abhkd->abhqd", attn_weights.astype(jnp.float32), values_all
    ).astype(jnp.bfloat16)
    mixed_out = mixed_out.reshape(lat_windows, lon_windows, head_count, WLAT, WLON, head_size)
    return mixed_out.transpose(0, 3, 1, 4, 2, 5).reshape(
        row_count, col_count, head_count * head_size
    )


def block_forward(rolled, gains, weight_qkv, weight_proj, row_offset, total_rows, head_count):
    normed = layer_norm(rolled.astype(jnp.float32), gains).astype(jnp.bfloat16)
    packed = jnp.dot(normed, weight_qkv, preferred_element_type=jnp.float32).astype(jnp.bfloat16)
    mixed_out = window_attention(packed, row_offset, total_rows, head_count)
    added = jnp.dot(mixed_out, weight_proj, preferred_element_type=jnp.float32)
    result = (rolled.astype(jnp.float32) + added).astype(jnp.bfloat16)
    return (result, (normed, packed, mixed_out))


def block_backward(
    grad_out, rolled, gains, weight_qkv, weight_proj, saved, row_offset, total_rows, head_count
):
    normed, packed, mixed_out = saved
    grad_mixed = lax.dot_general(
        grad_out, weight_proj, (((2,), (1,)), ((), ())), preferred_element_type=jnp.float32
    ).astype(jnp.bfloat16)
    grad_proj = lax.dot_general(
        mixed_out, grad_out, (((0, 1), (0, 1)), ((), ())), preferred_element_type=jnp.float32
    )

    def attend_only(packed_in):
        return window_attention(packed_in, row_offset, total_rows, head_count)

    _, attend_back = jax.vjp(attend_only, packed)
    grad_packed = attend_back(grad_mixed)[0]
    grad_normed = lax.dot_general(
        grad_packed, weight_qkv, (((2,), (1,)), ((), ())), preferred_element_type=jnp.float32
    ).astype(jnp.bfloat16)
    grad_qkv = lax.dot_general(
        normed, grad_packed, (((0, 1), (0, 1)), ((), ())), preferred_element_type=jnp.float32
    )
    _, norm_back = jax.vjp(layer_norm, rolled.astype(jnp.float32), gains)
    grad_input, grad_gain = norm_back(grad_normed.astype(jnp.float32))
    grad_rolled = (grad_out.astype(jnp.float32) + grad_input).astype(jnp.bfloat16)
    return (grad_rolled, grad_gain, grad_qkv, grad_proj)


def merge_tokens(patch_grid):
    row_count, col_count, breadth = patch_grid.shape
    reshaped = patch_grid.reshape(row_count // 2, 2, col_count // 2, 2, breadth)
    return reshaped.transpose(0, 2, 3, 1, 4).reshape(row_count // 2, col_count // 2, 4 * breadth)


def split_tokens(merged_grid):
    row_count, col_count, breadth = merged_grid.shape
    narrow = breadth // 4
    reshaped = merged_grid.reshape(row_count, col_count, 2, 2, narrow)
    return reshaped.transpose(0, 3, 1, 2, 4).reshape(2 * row_count, 2 * col_count, narrow)


def merge_forward(fine_grid, gains, weight):
    packed_grid = merge_tokens(fine_grid)
    normed = layer_norm(packed_grid.astype(jnp.float32), gains).astype(jnp.bfloat16)
    merged = jnp.dot(normed, weight, preferred_element_type=jnp.float32).astype(jnp.bfloat16)
    return (merged, (packed_grid, normed))


def merge_backward(grad_merged, saved, gains, weight):
    packed_grid, normed = saved
    grad_normed = lax.dot_general(
        grad_merged, weight, (((2,), (1,)), ((), ())), preferred_element_type=jnp.float32
    ).astype(jnp.bfloat16)
    grad_weight = lax.dot_general(
        normed, grad_merged, (((0, 1), (0, 1)), ((), ())), preferred_element_type=jnp.float32
    )
    _, norm_back = jax.vjp(layer_norm, packed_grid.astype(jnp.float32), gains)
    grad_packed, grad_gain = norm_back(grad_normed.astype(jnp.float32))
    return (split_tokens(grad_packed.astype(jnp.bfloat16)), grad_gain, grad_weight)


def rotate_ahead(patch_grid):
    arrived = from_behind(patch_grid[:SLAT], "lat", -1)
    patch_grid = jnp.concatenate([patch_grid[SLAT:], arrived], axis=0)
    arrived = from_behind(patch_grid[:, :SLON], "lon", -1)
    return jnp.concatenate([patch_grid[:, SLON:], arrived], axis=1)


def rotate_back(patch_grid):
    arrived = from_behind(patch_grid[-SLAT:], "lat", 1)
    patch_grid = jnp.concatenate([arrived, patch_grid[:-SLAT]], axis=0)
    arrived = from_behind(patch_grid[:, -SLON:], "lon", 1)
    return jnp.concatenate([arrived, patch_grid[:, :-SLON]], axis=1)


def local(
    tokens,
    fine_gain,
    fine_qkv,
    fine_proj,
    merge_gain,
    merge_weight,
    coarse_gain,
    coarse_qkv,
    coarse_proj,
    cotangent,
):
    fine_rows = tokens.shape[0]
    coarse_rows = fine_rows // 2
    lat_count = lax.axis_size("lat")
    lat_place = lax.axis_index("lat")
    fine_total = fine_rows * lat_count
    coarse_total = coarse_rows * lat_count
    fine_offset = lat_place * fine_rows
    coarse_offset = lat_place * coarse_rows
    grad_scale = (fine_total * tokens.shape[1] * lax.axis_size("lon") // 4) ** (-0.5)
    rolled_fine = rotate_ahead(tokens)
    fine_result, fine_saved = block_forward(
        rolled_fine, fine_gain, fine_qkv, fine_proj, fine_offset, fine_total, HF
    )
    fine_grid = rotate_back(fine_result)
    merged, merge_saved = merge_forward(fine_grid, merge_gain, merge_weight)
    rolled_coarse = rotate_ahead(merged)
    coarse_result, coarse_saved = block_forward(
        rolled_coarse, coarse_gain, coarse_qkv, coarse_proj, coarse_offset, coarse_total, HC
    )
    output = rotate_back(coarse_result)
    grad_coarse_out = rotate_ahead(cotangent)
    grad_rolled_coarse, coarse_gain_sum, coarse_qkv_sum, coarse_proj_sum = block_backward(
        grad_coarse_out,
        rolled_coarse,
        coarse_gain,
        coarse_qkv,
        coarse_proj,
        coarse_saved,
        coarse_offset,
        coarse_total,
        HC,
    )
    grad_merged = rotate_back(grad_rolled_coarse)
    grad_fine_grid, merge_gain_sum, merge_weight_sum = merge_backward(
        grad_merged, merge_saved, merge_gain, merge_weight
    )
    grad_fine_out = rotate_ahead(grad_fine_grid)
    grad_rolled_fine, fine_gain_sum, fine_qkv_sum, fine_proj_sum = block_backward(
        grad_fine_out,
        rolled_fine,
        fine_gain,
        fine_qkv,
        fine_proj,
        fine_saved,
        fine_offset,
        fine_total,
        HF,
    )
    grad_tokens = rotate_back(grad_rolled_fine)
    summed = (
        lax.psum_scatter(fine_gain_sum, ("lat", "lon"), scatter_dimension=0, tiled=True),
        lax.psum_scatter(fine_qkv_sum, ("lat", "lon"), scatter_dimension=0, tiled=True),
        lax.psum_scatter(fine_proj_sum, ("lat", "lon"), scatter_dimension=0, tiled=True),
        lax.psum_scatter(merge_gain_sum, ("lat", "lon"), scatter_dimension=0, tiled=True),
        lax.psum_scatter(merge_weight_sum, ("lat", "lon"), scatter_dimension=0, tiled=True),
        lax.psum_scatter(coarse_gain_sum, ("lat", "lon"), scatter_dimension=0, tiled=True),
        lax.psum_scatter(coarse_qkv_sum, ("lat", "lon"), scatter_dimension=0, tiled=True),
        lax.psum_scatter(coarse_proj_sum, ("lat", "lon"), scatter_dimension=0, tiled=True),
    )
    fine_gain_sum, fine_qkv_sum, fine_proj_sum = (summed[0], summed[1], summed[2])
    merge_gain_sum, merge_weight_sum = (summed[3], summed[4])
    coarse_gain_sum, coarse_qkv_sum, coarse_proj_sum = (summed[5], summed[6], summed[7])
    return (
        output,
        grad_tokens,
        fine_gain_sum * grad_scale,
        fine_qkv_sum * grad_scale,
        fine_proj_sum * grad_scale,
        merge_gain_sum * grad_scale,
        merge_weight_sum * grad_scale,
        coarse_gain_sum * grad_scale,
        coarse_qkv_sum * grad_scale,
        coarse_proj_sum * grad_scale,
    )


def solution(mesh):
    return jax.shard_map(
        local,
        mesh=mesh,
        in_specs=(
            P("lat", "lon", None),
            P(),
            P(),
            P(),
            P(),
            P(),
            P(),
            P(),
            P(),
            P("lat", "lon", None),
        ),
        out_specs=(
            P("lat", "lon", None),
            P("lat", "lon", None),
            P(("lat", "lon")),
            P(("lat", "lon"), None),
            P(("lat", "lon"), None),
            P(("lat", "lon")),
            P(("lat", "lon"), None),
            P(("lat", "lon")),
            P(("lat", "lon"), None),
            P(("lat", "lon"), None),
        ),
        check_vma=False,
    )
```

profile of v0, /device:TPU:0, one launch (start us, length us, event | category | flops | bytes accessed | tf_op | source)
XLA Modules:
  0.0 741.3 jit_solution(9784715575676584842)
XLA Ops:
  8.3 5.1 collective-permute-start
  34.3 4.6 collective-permute-done.2
  39.6 4.2 collective-permute-done.3
  52.6 2.6 collective-permute-done.4
  58.3 2.6 convolution_convert_fusion.1
  83.4 5.9 collective-permute-done.10
  89.4 4.4 collective-permute-done.11
  104.7 2.9 collective-permute-done.12
  117.9 2.2 convolution_bitcast_fusion.3
  130.9 2.3 copy.145
  133.3 2.4 copy.146
  135.7 2.6 reshape.394
  138.3 3.0 convolution_bitcast_fusion.2
  141.6 3.3 convolution_bitcast_fusion
  145.8 2.8 convolution_bitcast_fusion.1
  149.9 5.9 collective-permute-done.6
  155.9 4.4 collective-permute-done.7
  163.7 39.3 %all-reduce.9 = (f32[512]{0:T(512)S(1)}, f32[2048]{0:T(1024)S(1)}, f32[512]{0:T(512)S(1)}) all-reduce(f32[512]{0:T(512)S(1)} %get-tuple-element.12, f32[2048]{0:T(1024)S(1)} %copy-done.58, f32[512]{0:T(512)S(1)} %copy-done.61), channel_id=2, replica_groups=mesh['lat'=4,'lon'=8] {'lat','lon'}, use_global_device_ids=true, to_apply=%region_23.24.clone | all-reduce | flops 3072 | bytes 24576
  204.3 4.4 collective-permute-done.15
  209.5 39.5 %reduce-scatter.8.cloned.1.call-done = f32[8,512]{1,0:T(8,128)} async-done(((f32[256,512]{1,0:T(8,128)}), f32[8,512]{1,0:T(8,128)}) %reduce-scatter.8.cloned.1.call-update) | async-done | bytes 16400 | tf_op jit(solution)/shard_map/reduce_scatter | solution.py:210
  250.3 133.4 %reduce-scatter.14.cloned.1.call-done = f32[16,512]{1,0:T(8,128)} async-done(((f32[512,512]{1,0:T(8,128)}), f32[16,512]{1,0:T(8,128)}) %reduce-scatter.14.cloned.1.call-update) | async-done | bytes 32784 | tf_op jit(solution)/shard_map/reduce_scatter | solution.py:215
  385.1 97.7 %reduce-scatter.6.cloned.1.call-done = f32[16,768]{1,0:T(8,128)} async-done(((f32[512,768]{1,0:T(8,128)}), f32[16,768]{1,0:T(8,128)}) %reduce-scatter.6.cloned.1.call-update) | async-done | bytes 49168 | tf_op jit(solution)/shard_map/reduce_scatter | solution.py:209
  484.3 105.1 %reduce-scatter.12.cloned.1.call-done = f32[16,1536]{1,0:T(8,128)} async-done(((f32[512,1536]{1,0:T(8,128)}), f32[16,1536]{1,0:T(8,128)}) %reduce-scatter.12.cloned.1.call-update) | async-done | bytes 98320 | tf_op jit(solution)/shard_map/reduce_scatter | solution.py:214
  590.9 142.2 %reduce-scatter.10.cloned.1.call-done = f32[64,512]{1,0:T(8,128)} async-done(((f32[2048,512]{1,0:T(8,128)}), f32[64,512]{1,0:T(8,128)}) %reduce-scatter.10.cloned.1.call-update) | async-done | bytes 131088 | tf_op jit(solution)/shard_map/reduce_scatter | solution.py:212
  (285 shorter events, 103.5 us)
Async XLA Ops:
  7.2 43.3 %copy-start = (bf16[2048,512]{1,0:T(8,128)(2,1)S(1)}, bf16[2048,512]{1,0:T(8,128)(2,1)}, u32[]{:S(2)}) copy-start(bf16[2048,512]{1,0:T(8,128)(2,1)} %param.15) | copy-start | bytes 6291460
  7.2 15.1 %copy-start.59 = (f32[512]{0:T(512)S(1)}, f32[512]{0:T(512)}, u32[]{:S(2)}) copy-start(f32[512]{0:T(512)} %param.11) | copy-start | bytes 6148
  7.2 241.8 %reduce-scatter.8.cloned.1.call-start = ((), (), s32[]{:S(2)}) async-start(), calls=%async_computation.6 | async-start | bytes 540672 | tf_op jit(solution)/shard_map/reduce_scatter | solution.py:210
  8.3 8.8 %collective-permute-start = (bf16[3,24,512]{2,1,0:T(8,128)(2,1)S(1)}, bf16[3,24,512]{2,1,0:T(8,128)(2,1)S(1)}, u32[]{:S(2)}, u32[]{:S(2)}) collective-permute-start(bf16[3,24,512]{2,1,0:T(8,128)(2,1)S(1)} %slice.127), channel_id=1, source_target_pairs={{0,24},{8,0},{16,8},{24,16},{1,25},{9,1},{17,9},{25,17},{2,26},{10... | collective-permute-start | bytes 221192 | tf_op jit(solution)/shard_map/ppermute | solution.py:20
  14.8 36.8 %collective-permute-start.8 = (bf16[3,12,512]{2,1,0:T(8,128)(2,1)}, bf16[3,12,512]{2,1,0:T(8,128)(2,1)}, u32[]{:S(2)}, u32[]{:S(2)}) collective-permute-start(bf16[3,12,512]{2,1,0:T(8,128)(2,1)} %get-tuple-element.42), channel_id=1, source_target_pairs={{0,24},{8,0},{16,8},{24,16},{1,25},{9,1},{17,9},{25,17},{2,26},{10... | collective-permute-start | bytes 110600 | tf_op jit(solution)/shard_map/ppermute | solution.py:20
  17.2 3.6 collective-permute-start.1
  31.2 15.3 %copy-start.16 = (bf16[12,24,256]{2,1,0:T(8,128)(2,1)}, bf16[12,24,256]{2,1,0:T(8,128)(2,1)S(1)}, u32[]{:S(2)}) copy-start(bf16[12,24,256]{2,1,0:T(8,128)(2,1)S(1)} %reshape.378) | copy-start | bytes 442372
  32.5 6.4 collective-permute-start.2
  38.9 5.0 collective-permute-start.3
  51.1 4.1 collective-permute-start.4
  52.5 3.3 collective-permute-start.9
  55.9 2.1 collective-permute-start.5
  83.3 5.9 collective-permute-start.10
  89.3 4.5 collective-permute-start.11
  103.2 4.4 collective-permute-start.12
  107.6 2.3 collective-permute-start.13
  112.6 271.1 %reduce-scatter.14.cloned.1.call-start = ((), (), s32[]{:S(2)}) async-start(), calls=%async_computation.9 | async-start | bytes 1081344 | tf_op jit(solution)/shard_map/reduce_scatter | solution.py:215
  120.1 362.8 %reduce-scatter.6.cloned.1.call-start = ((), (), s32[]{:S(2)}) async-start(), calls=%async_computation.5 | async-start | bytes 1622016 | tf_op jit(solution)/shard_map/reduce_scatter | solution.py:209
  141.3 448.1 %reduce-scatter.12.cloned.1.call-start = ((), (), s32[]{:S(2)}) async-start(), calls=%async_computation.8 | async-start | bytes 3244032 | tf_op jit(solution)/shard_map/reduce_scatter | solution.py:214
  145.0 588.2 %reduce-scatter.10.cloned.1.call-start = ((), (), s32[]{:S(2)}) async-start(), calls=%async_computation.7 | async-start | bytes 4325376 | tf_op jit(solution)/shard_map/reduce_scatter | solution.py:212
  149.8 6.0 collective-permute-start.6
  155.9 4.5 collective-permute-start.7
  163.6 39.9 %collective-permute-start.14 = (bf16[3,24,512]{2,1,0:T(8,128)(2,1)S(1)}, bf16[3,24,512]{2,1,0:T(8,128)(2,1)S(1)}, u32[]{:S(2)}, u32[]{:S(2)}) collective-permute-start(bf16[3,24,512]{2,1,0:T(8,128)(2,1)S(1)} %slice.192), channel_id=1, source_target_pairs={{0,8},{8,16},{16,24},{24,0},{1,9},{9,17},{17,25},{25,1},{2,10},{10... | collective-permute-start | bytes 221192 | tf_op jit(solution)/shard_map/ppermute | solution.py:20
  203.6 5.1 collective-permute-start.15
  (59 other events, 236.7 us)
Sparse Core Ops, SparseCore 0:
  112.7 136.2 reduce-scatter.7
  251.3 132.4 reduce-scatter.13
  389.0 93.8 reduce-scatter.5
  488.1 101.1 reduce-scatter.11
  591.5 141.6 reduce-scatter.9
where the time goes:
time: 743 us; the launch traced here: 741 us
  waiting for transfers between devices  562 us (76%)
  local copies, waits for them, and re-layouts  55 us (7%)
  blocking collectives  39.3 us (5%)
  matrix products  36.7 us (5%)
  other arithmetic  22.9 us (3%)
  between operations  14.9 us (2%)
  starting transfers between devices  10.6 us (1%)
    reduce_scatter x1, waiting for transfers between devices, local(): lax.psum_scatter(merge_weight_sum, ('lat', 'lon'), scatter_dimension=0, t...  142 us
    reduce_scatter x1, waiting for transfers between devices, local(): lax.psum_scatter(coarse_proj_sum, ('lat', 'lon'), scatter_dimension=0, ti...  133 us
    reduce_scatter x1, waiting for transfers between devices, local(): lax.psum_scatter(coarse_qkv_sum, ('lat', 'lon'), scatter_dimension=0, til...  105 us
    reduce_scatter x1, waiting for transfers between devices, local(): lax.psum_scatter(fine_qkv_sum, ('lat', 'lon'), scatter_dimension=0, tiled...  97.7 us
    ppermute x16, waiting for transfers between devices, from_behind(): return lax.ppermute(value, axis, pairs)  43.7 us
    reduce_scatter x1, waiting for transfers between devices, local(): lax.psum_scatter(fine_proj_sum, ('lat', 'lon'), scatter_dimension=0, tile...  39.5 us
    unnamed x1, blocking collectives  39.3 us
  transfers between devices with their start and end apart: 21, of which 17 were waited for; matrix products, arithmetic and copies ran while one was open for 9% of the time, Pallas kernels for 0%

commit v1 on v0

--- a/solution.py
+++ b/solution.py
@@ -12,12 +12,6 @@
 
 
 EPSILON = 1e-05
-
-
-def from_behind(value, axis, steps):
-    count = lax.axis_size(axis)
-    pairs = [(source, (source + steps) % count) for source in range(count)]
-    return lax.ppermute(value, axis, pairs)
 
 
 def layer_norm(values, gains):
@@ -129,18 +123,76 @@
     return (split_tokens(grad_packed.astype(jnp.bfloat16)), grad_gain, grad_weight)
 
 
-def rotate_ahead(patch_grid):
-    arrived = from_behind(patch_grid[:SLAT], "lat", -1)
-    patch_grid = jnp.concatenate([patch_grid[SLAT:], arrived], axis=0)
-    arrived = from_behind(patch_grid[:, :SLON], "lon", -1)
-    return jnp.concatenate([patch_grid[:, SLON:], arrived], axis=1)
-
-
-def rotate_back(patch_grid):
-    arrived = from_behind(patch_grid[-SLAT:], "lat", 1)
-    patch_grid = jnp.concatenate([arrived, patch_grid[:-SLAT]], axis=0)
-    arrived = from_behind(patch_grid[:, -SLON:], "lon", 1)
-    return jnp.concatenate([arrived, patch_grid[:, :-SLON]], axis=1)
+def shift_pairs(lat_step, lon_step):
+    lats, lons = lax.axis_size("lat"), lax.axis_size("lon")
+    return [
+        (a * lons + b, ((a + lat_step) % lats) * lons + (b + lon_step) % lons)
+        for a in range(lats)
+        for b in range(lons)
+    ]
+
+
+def send(value, lat_step, lon_step):
+    return lax.ppermute(value, ("lat", "lon"), shift_pairs(lat_step, lon_step))
+
+
+def rotate_ahead(grid):
+    below = send(grid[:SLAT, SLON:], -1, 0)
+    beside = send(grid[SLAT:, :SLON], 0, -1)
+    corner = send(grid[:SLAT, :SLON], -1, -1)
+    top = jnp.concatenate([grid[SLAT:, SLON:], beside], axis=1)
+    return jnp.concatenate([top, jnp.concatenate([below, corner], axis=1)], axis=0)
+
+
+def rotate_back(grid):
+    above = send(grid[-SLAT:, :-SLON], 1, 0)
+    beside = send(grid[:-SLAT, -SLON:], 0, 1)
+    corner = send(grid[-SLAT:, -SLON:], 1, 1)
+    low = jnp.concatenate([beside, grid[:-SLAT, :-SLON]], axis=1)
+    return jnp.concatenate([jnp.concatenate([corner, above], axis=1), low], axis=0)
+
+
+def halve(value, axis, step):
+    count = lax.axis_size(axis)
+    bit = (lax.axis_index(axis) // step) % 2
+    kept = lax.dynamic_index_in_dim(value, bit, 1, keepdims=False)
+    gone = lax.dynamic_index_in_dim(value, 1 - bit, 1, keepdims=False)
+    came = lax.ppermute(gone, axis, [(i, i ^ step) for i in range(count)])
+    return (kept.astype(jnp.float32) + came.astype(jnp.float32)).astype(value.dtype)
+
+
+def reduce_pieces(value):
+    lats, lons = lax.axis_size("lat"), lax.axis_size("lon")
+    rows, columns = value.shape[1:]
+    if lats & (lats - 1) or lons & (lons - 1):
+        total = lax.psum_scatter(value, ("lat", "lon"), scatter_dimension=0, tiled=True)
+        return total.reshape(rows, columns)
+    step = 1
+    while step < lons:
+        left = lons // step
+        value = value.reshape(lats * left // 2, 2, rows, columns)
+        value = halve(value, "lon", step)
+        step *= 2
+    step = 1
+    while step < lats:
+        left = lats // step
+        value = value.reshape(left // 2, 2, rows, columns)
+        value = halve(value, "lat", step)
+        step *= 2
+    return value.reshape(rows, columns)
+
+
+def as_pieces(value, devices, width):
+    rows = value.shape[0] // devices
+    value = value.astype(jnp.bfloat16).reshape(devices, rows, value.shape[1])
+    parts = [value[:, :, i : i + width] for i in range(0, value.shape[2], width)]
+    return jnp.concatenate(parts, axis=1)
+
+
+def from_pieces(value, rows, columns):
+    width = value.shape[1]
+    parts = [value[i * rows : (i + 1) * rows] for i in range(columns // width)]
+    return jnp.concatenate(parts, axis=1).astype(jnp.float32)
 
 
 def local(
@@ -168,9 +220,9 @@
     fine_result, fine_saved = block_forward(
         rolled_fine, fine_gain, fine_qkv, fine_proj, fine_offset, fine_total, HF
     )
-    fine_grid = rotate_back(fine_result)
+    fine_grid = rotate_ahead(fine_result)
     merged, merge_saved = merge_forward(fine_grid, merge_gain, merge_weight)
-    rolled_coarse = rotate_ahead(merged)
+    rolled_coarse = merged
     coarse_result, coarse_saved = block_forward(
         rolled_coarse, coarse_gain, coarse_qkv, coarse_proj, coarse_offset, coarse_total, HC
     )
@@ -187,11 +239,11 @@
         coarse_total,
         HC,
     )
-    grad_merged = rotate_back(grad_rolled_coarse)
+    grad_merged = grad_rolled_coarse
     grad_fine_grid, merge_gain_sum, merge_weight_sum = merge_backward(
         grad_merged, merge_saved, merge_gain, merge_weight
     )
-    grad_fine_out = rotate_ahead(grad_fine_grid)
+    grad_fine_out = rotate_back(grad_fine_grid)
     grad_rolled_fine, fine_gain_sum, fine_qkv_sum, fine_proj_sum = block_backward(
         grad_fine_out,
         rolled_fine,
@@ -204,19 +256,27 @@
         HF,
     )
     grad_tokens = rotate_back(grad_rolled_fine)
-    summed = (
-        lax.psum_scatter(fine_gain_sum, ("lat", "lon"), scatter_dimension=0, tiled=True),
-        lax.psum_scatter(fine_qkv_sum, ("lat", "lon"), scatter_dimension=0, tiled=True),
-        lax.psum_scatter(fine_proj_sum, ("lat", "lon"), scatter_dimension=0, tiled=True),
-        lax.psum_scatter(merge_gain_sum, ("lat", "lon"), scatter_dimension=0, tiled=True),
-        lax.psum_scatter(merge_weight_sum, ("lat", "lon"), scatter_dimension=0, tiled=True),
-        lax.psum_scatter(coarse_gain_sum, ("lat", "lon"), scatter_dimension=0, tiled=True),
-        lax.psum_scatter(coarse_qkv_sum, ("lat", "lon"), scatter_dimension=0, tiled=True),
-        lax.psum_scatter(coarse_proj_sum, ("lat", "lon"), scatter_dimension=0, tiled=True),
-    )
-    fine_gain_sum, fine_qkv_sum, fine_proj_sum = (summed[0], summed[1], summed[2])
-    merge_gain_sum, merge_weight_sum = (summed[3], summed[4])
-    coarse_gain_sum, coarse_qkv_sum, coarse_proj_sum = (summed[5], summed[6], summed[7])
+    devices = lat_count * lax.axis_size("lon")
+
+    def gather_sums(sums, width):
+        pieces = [as_pieces(value, devices, width) for value in sums]
+        total = reduce_pieces(jnp.concatenate(pieces, axis=1))
+        found, start = [], 0
+        for value, piece in zip(sums, pieces):
+            part = total[start : start + piece.shape[1]]
+            found.append(from_pieces(part, value.shape[0] // devices, value.shape[1]))
+            start += piece.shape[1]
+        return found
+
+    merge_weight_sum, coarse_qkv_sum, coarse_proj_sum = gather_sums(
+        (merge_weight_sum, coarse_qkv_sum, coarse_proj_sum), coarse_proj.shape[1]
+    )
+    fine_qkv_sum, fine_proj_sum = gather_sums((fine_qkv_sum, fine_proj_sum), 256)
+    gains = [v.reshape(devices, -1) for v in (fine_gain_sum, merge_gain_sum, coarse_gain_sum)]
+    gain_sums = reduce_pieces(jnp.concatenate(gains, axis=1)[:, None, :])[0]
+    first, second = gains[0].shape[1], gains[0].shape[1] + gains[1].shape[1]
+    fine_gain_sum, merge_gain_sum = gain_sums[:first], gain_sums[first:second]
+    coarse_gain_sum = gain_sums[second:]
     return (
         output,
         grad_tokens,

time: 743 us -> 212 us (0.29)
  waiting for transfers between devices: 562 us -> 64.8 us
  blocking collectives: 39.3 us -> 0 us
  starting transfers between devices: 10.6 us -> 30.6 us
  between operations: 14.9 us -> 2.21 us
    reduce_scatter x5 -> x0, waiting for transfers between devices: 518 us -> none  [the longest x1 142 us: local(): lax.psum_scatter(merge_weight_sum, ('lat', 'lon'), scatter_dimension=0, t...]
    unnamed x1 -> x0, blocking collectives: 39.3 us -> none
    ppermute x16 -> x33, waiting for transfers between devices: 43.7 us -> 64.8 us  [the longest x15 58.5 us: halve(): came = lax.ppermute(gone, axis, [(i, i ^ step) for i in range(count)])]
    ppermute x16 -> x33, starting transfers between devices: 10.2 us -> 30.6 us  [the longest x18 19.9 us: send(): return lax.ppermute(value, ('lat', 'lon'), shift_pairs(lat_step, lon_step))]
  transfers between devices with their start and end apart: 21 -> 33, of which waited for: 17 -> 14; matrix products, arithmetic and copies ran while one was open for 9% -> 24% of each run, Pallas kernels for 0% -> 0%
where the time goes in v1:
time: 212 us; the launch traced here: 211 us
  waiting for transfers between devices  64.8 us (31%)
  local copies, waits for them, and re-layouts  57.4 us (27%)
  starting transfers between devices  30.6 us (14%)
  matrix products  30.6 us (14%)
  other arithmetic  25 us (12%)
  between operations  2.21 us (1%)
    ppermute x15, waiting for transfers between devices, halve(): came = lax.ppermute(gone, axis, [(i, i ^ step) for i in range(count)])  58.5 us
    ppermute x18, starting transfers between devices, send(): return lax.ppermute(value, ('lat', 'lon'), shift_pairs(lat_step, lon_step))  19.9 us
    unnamed x140, local copies, waits for them, and re-layouts  10.9 us
    ppermute x15, starting transfers between devices, halve(): came = lax.ppermute(gone, axis, [(i, i ^ step) for i in range(count)])  10.7 us
    reshape x6, local copies, waits for them, and re-layouts, window_attention(): packed.reshape(lat_windows, WLAT, lon_windows, WLON, 3, head_count, head_...  9.33 us
    ppermute x18, waiting for transfers between devices, send(): return lax.ppermute(value, ('lat', 'lon'), shift_pairs(lat_step, lon_step))  6.32 us
    dot_general x6, matrix products, window_attention(): jnp.einsum('abhqk,abhkd->abhqd', attn_weights.astype(jnp.float32), values...  4.99 us
    another operation x4, local copies, waits for them, and re-layouts  4.97 us
  transfers between devices with their start and end apart: 33, of which 14 were waited for; matrix products, arithmetic and copies ran while one was open for 24% of the time, Pallas kernels for 0%

profile of v1, /device:TPU:0, one launch (start us, length us, event | category | flops | bytes accessed | tf_op | source)
XLA Modules:
  0.0 210.7 jit_solution(1381845734558303194)
XLA Ops:
  2.2 6.4 %collective-permute-start.2 = (bf16[3,6,512]{2,1,0:T(8,128)(2,1)}, bf16[3,6,512]{2,1,0:T(8,128)(2,1)}, u32[]{:S(2)}, u32[]{:S(2)}) collective-permute-start(bf16[3,6,512]{2,1,0:T(8,128)(2,1)} %slice.211), channel_id=1, source_target_pairs={{0,31},{1,24},{2,25},{3,26},{4,27},{5,28},{6,29},{7,30},{8,7},{9,0... | collective-permute-start | bytes 55304 | tf_op jit(solution)/shard_map/ppermute | solution.py:136
  31.1 4.7 %collective-permute-start.5 = (bf16[3,6,512]{2,1,0:T(8,128)(2,1)S(1)}, bf16[3,6,512]{2,1,0:T(8,128)(2,1)S(1)}, u32[]{:S(2)}, u32[]{:S(2)}) collective-permute-start(bf16[3,6,512]{2,1,0:T(8,128)(2,1)S(1)} %slice.273), channel_id=1, source_target_pairs={{0,31},{1,24},{2,25},{3,26},{4,27},{5,28},{6,29},{7,30},{8,7},{9,0... | collective-permute-start | bytes 55304 | tf_op jit(solution)/shard_map/ppermute | solution.py:136
  37.3 2.8 %collective-permute-done.4 = bf16[3,18,512]{2,1,0:T(8,128)(2,1)S(1)} collective-permute-done((bf16[3,18,512]{2,1,0:T(8,128)(2,1)S(1)}, bf16[3,18,512]{2,1,0:T(8,128)(2,1)S(1)}, u32[]{:S(2)}, u32[]{:S(2)}) %collective-permute-start.4) | collective-permute-done | bytes 55328 | tf_op jit(solution)/shard_map/ppermute | solution.py:136
  49.9 2.0 reshape.505
  63.2 2.0 copy.171
  67.1 2.0 reshape.514
  69.2 2.2 %multiply_reduce_fusion.6 = (f32[6,12]{1,0:T(8,128)S(1)}, f32[6,12,512]{2,1,0:T(8,128)S(1)}) fusion(f32[6,12,512]{2,1,0:T(8,128)S(1)} %get-tuple-element.64, f32[512]{0:T(512)S(1)} %copy-done.52, f32[6,12]{1,0:T(8,128)S(1)} %broadcast_multiply_fusion.1, bf16[6,12,1536]{2,1,0:T(8,128)(2,1)} %reshape.514, bf16[512,1536]{1,0:T(8,128)(2,1)} %param.17), kind=kOutput, calls=%fused_computation.138 | convolution fusion | flops 113467320 | bytes 2091584 | tf_op jit(solution)/shard_map/dot_general | solution.py:81
  72.3 2.3 %multiply_reduce_fusion.1 = (f32[6,12]{1,0:T(8,128)}, f32[6,12,2048]{2,1,0:T(8,128)}) fusion(f32[6,12,2048]{2,1,0:T(8,128)S(1)} %reshape.534, f32[2048]{0:T(1024)S(1)} %copy-done.27, f32[6,12]{1,0:T(8,128)S(1)} %broadcast_multiply_fusion.2, bf16[6,12,512]{2,1,0:T(8,128)(2,1)S(1)} %add_convert_fusion.3, bf16[2048,512]{1,0:T(8,128)(2,1)S(1)} %copy-done), kind=kOutput, calls=%fused_computation.77 | convolution fusion | flops 151879616 | bytes 3359296 | tf_op jit(solution)/shard_map/dot_general | solution.py:115
  74.6 2.2 %bitcast_convert_fusion = bf16[2048,512]{1,0:T(8,128)(2,1)} fusion(bf16[6,12,512]{2,1,0:T(8,128)(2,1)S(1)} %add_convert_fusion.3, f32[6,12,2048]{2,1,0:T(8,128)S(1)} %reshape.534, f32[2048]{0:T(1024)S(1)} %copy-done.27, f32[6,12]{1,0:T(8,128)S(1)} %copy-done.43, f32[6,12]{1,0:T(8,128)S(1)} %broadcast_multiply_fusion.2), kind=kOutput, calls=%fused_computation.2 | convolution fusion | flops 152633344 | bytes 2769472 | tf_op jit(solution)/shard_map/dot_general | solution.py:118
  83.6 2.2 %multiply_reduce_fusion = (f32[2048]{0:T(1024)}, f32[6,12]{1,0:T(8,128)S(1)}) fusion(f32[6,12,2048]{2,1,0:T(8,128)} %get-tuple-element.71, f32[6,12,2048]{2,1,0:T(8,128)S(1)} %reshape.534, f32[6,12]{1,0:T(8,128)} %copy-done.42, f32[6,12]{1,0:T(8,128)S(1)} %broadcast_multiply_fusion.2, f32[6,12]{1,0:T(8,128)S(1)} %multiply_multiply_fusion.1, ...), kind=kLoop, calls=%fused_computation.74 | loop fusion | flops 1472440 | bytes 1197184 | tf_op jit(solution)/shard_map/transpose(jvp())/reduce_sum | solution.py:21
  101.0 2.3 %collective-permute-start.12 = (bf16[3,6,512]{2,1,0:T(8,128)(2,1)}, bf16[3,6,512]{2,1,0:T(8,128)(2,1)S(1)}, u32[]{:S(2)}, u32[]{:S(2)}) collective-permute-start(bf16[3,6,512]{2,1,0:T(8,128)(2,1)} %slice.281), channel_id=1, source_target_pairs={{0,9},{1,10},{2,11},{3,12},{4,13},{5,14},{6,15},{7,8},{8,17},{9,18... | collective-permute-start | bytes 55304 | tf_op jit(solution)/shard_map/ppermute | solution.py:136
  105.0 3.0 %collective-permute-done.12 = bf16[3,6,512]{2,1,0:T(8,128)(2,1)S(1)} collective-permute-done((bf16[3,6,512]{2,1,0:T(8,128)(2,1)}, bf16[3,6,512]{2,1,0:T(8,128)(2,1)S(1)}, u32[]{:S(2)}, u32[]{:S(2)}) %collective-permute-start.12) | collective-permute-done | bytes 18464 | tf_op jit(solution)/shard_map/ppermute | solution.py:136
  133.0 3.1 %collective-permute-done.19 = f32[8,1,96]{2,0,1:T(8,128)S(1)} collective-permute-done((f32[8,1,96]{2,0,1:T(8,128)S(1)}, f32[8,1,96]{2,0,1:T(8,128)S(1)}, u32[]{:S(2)}, u32[]{:S(2)}) %collective-permute-start.19) | collective-permute-done | bytes 3104 | tf_op jit(solution)/shard_map/ppermute | solution.py:160
  137.5 2.2 %collective-permute-done.20 = f32[4,1,96]{2,0,1:T(4,128)S(1)} collective-permute-done((f32[4,1,96]{2,0,1:T(4,128)S(1)}, f32[4,1,96]{2,0,1:T(4,128)S(1)}, u32[]{:S(2)}, u32[]{:S(2)}) %collective-permute-start.20) | collective-permute-done | bytes 1568 | tf_op jit(solution)/shard_map/ppermute | solution.py:160
  140.0 3.4 %collective-permute-done.21 = f32[2,1,96]{2,1,0:T(1,128)S(1)} collective-permute-done((f32[2,1,96]{2,1,0:T(1,128)S(1)}, f32[2,1,96]{2,1,0:T(1,128)S(1)}, u32[]{:S(2)}, u32[]{:S(2)}) %collective-permute-start.21) | collective-permute-done | bytes 800 | tf_op jit(solution)/shard_map/ppermute | solution.py:160
  145.1 2.9 %collective-permute-done.22 = f32[1,1,96]{2,1,0:T(1,128)S(1)} collective-permute-done((f32[1,1,96]{2,1,0:T(1,128)S(1)}, f32[1,1,96]{2,1,0:T(1,128)S(1)}, u32[]{:S(2)}, u32[]{:S(2)}) %collective-permute-start.22) | collective-permute-done | bytes 416 | tf_op jit(solution)/shard_map/ppermute | solution.py:160
  150.0 2.2 %fusion = bf16[16,128,512]{2,1,0:T(8,128)(2,1)S(1)} fusion(bf16[16,128,512]{2,1,0:T(8,128)(2,1)} %collective-permute-done.28, bf16[16,2,128,512]{3,2,1,0:T(8,128)(2,1)S(1)} %copy-done.2, s32[]{:T(128)S(6)} %select_n.157), kind=kLoop, calls=%fused_computation.1 | loop fusion | flops 4194304 | bytes 6291460 | tf_op jit(solution)/shard_map/convert_element_type | solution.py:161
  153.3 4.4 %collective-permute-done.24 = bf16[8,64,256]{2,1,0:T(8,128)(2,1)S(1)} collective-permute-done((bf16[8,64,256]{2,1,0:T(8,128)(2,1)S(1)}, bf16[8,64,256]{2,1,0:T(8,128)(2,1)S(1)}, u32[]{:S(2)}, u32[]{:S(2)}) %collective-permute-start.24) | collective-permute-done | bytes 262176 | tf_op jit(solution)/shard_map/ppermute | solution.py:160
  159.8 3.0 %collective-permute-done.25 = bf16[4,64,256]{2,1,0:T(8,128)(2,1)S(1)} collective-permute-done((bf16[4,64,256]{2,1,0:T(8,128)(2,1)S(1)}, bf16[4,64,256]{2,1,0:T(8,128)(2,1)S(1)}, u32[]{:S(2)}, u32[]{:S(2)}) %collective-permute-start.25) | collective-permute-done | bytes 131104 | tf_op jit(solution)/shard_map/ppermute | solution.py:160
  163.0 16.9 %collective-permute-done.29 = bf16[8,128,512]{2,1,0:T(8,128)(2,1)S(1)} collective-permute-done((bf16[8,128,512]{2,1,0:T(8,128)(2,1)S(1)}, bf16[8,128,512]{2,1,0:T(8,128)(2,1)S(1)}, u32[]{:S(2)}, u32[]{:S(2)}) %collective-permute-start.29) | collective-permute-done | bytes 1048608 | tf_op jit(solution)/shard_map/ppermute | solution.py:160
  183.3 3.0 %collective-permute-done.27 = bf16[1,64,256]{2,1,0:T(8,128)(2,1)S(1)} collective-permute-done((bf16[1,64,256]{2,1,0:T(8,128)(2,1)S(1)}, bf16[1,64,256]{2,1,0:T(8,128)(2,1)S(1)}, u32[]{:S(2)}, u32[]{:S(2)}) %collective-permute-start.27) | collective-permute-done | bytes 32800 | tf_op jit(solution)/shard_map/ppermute | solution.py:160
  186.4 7.5 %collective-permute-done.30 = bf16[4,128,512]{2,1,0:T(8,128)(2,1)S(1)} collective-permute-done((bf16[4,128,512]{2,1,0:T(8,128)(2,1)S(1)}, bf16[4,128,512]{2,1,0:T(8,128)(2,1)S(1)}, u32[]{:S(2)}, u32[]{:S(2)}) %collective-permute-start.30) | collective-permute-done | bytes 524320 | tf_op jit(solution)/shard_map/ppermute | solution.py:160
  194.5 6.7 %collective-permute-done.31 = bf16[2,128,512]{2,1,0:T(8,128)(2,1)S(1)} collective-permute-done((bf16[2,128,512]{2,1,0:T(8,128)(2,1)S(1)}, bf16[2,128,512]{2,1,0:T(8,128)(2,1)S(1)}, u32[]{:S(2)}, u32[]{:S(2)}) %collective-permute-start.31) | collective-permute-done | bytes 262176 | tf_op jit(solution)/shard_map/ppermute | solution.py:160
  203.4 5.3 %collective-permute-done.32 = bf16[1,128,512]{2,1,0:T(8,128)(2,1)S(1)} collective-permute-done((bf16[1,128,512]{2,1,0:T(8,128)(2,1)S(1)}, bf16[1,128,512]{2,1,0:T(8,128)(2,1)S(1)}, u32[]{:S(2)}, u32[]{:S(2)}) %collective-permute-start.32) | collective-permute-done | bytes 131104 | tf_op jit(solution)/shard_map/ppermute | solution.py:160
  (354 shorter events, 113.5 us)
Async XLA Ops:
  2.2 17.3 %collective-permute-start.2 = (bf16[3,6,512]{2,1,0:T(8,128)(2,1)}, bf16[3,6,512]{2,1,0:T(8,128)(2,1)}, u32[]{:S(2)}, u32[]{:S(2)}) collective-permute-start(bf16[3,6,512]{2,1,0:T(8,128)(2,1)} %slice.211), channel_id=1, source_target_pairs={{0,31},{1,24},{2,25},{3,26},{4,27},{5,28},{6,29},{7,30},{8,7},{9,0... | collective-permute-start | bytes 55304 | tf_op jit(solution)/shard_map/ppermute | solution.py:136
  9.5 10.0 %collective-permute-start.1 = (bf16[3,18,512]{2,1,0:T(8,128)(2,1)S(1)}, bf16[3,18,512]{2,1,0:T(8,128)(2,1)}, u32[]{:S(2)}, u32[]{:S(2)}) collective-permute-start(bf16[3,18,512]{2,1,0:T(8,128)(2,1)S(1)} %slice.210), channel_id=1, source_target_pairs={{0,24},{1,25},{2,26},{3,27},{4,28},{5,29},{6,30},{7,31},{8,0},{9,1... | collective-permute-start | bytes 165896 | tf_op jit(solution)/shard_map/ppermute | solution.py:136
  10.9 4.8 %collective-permute-start.11 = (bf16[3,6,512]{2,1,0:T(8,128)(2,1)S(1)}, bf16[3,6,512]{2,1,0:T(8,128)(2,1)S(1)}, u32[]{:S(2)}, u32[]{:S(2)}) collective-permute-start(bf16[3,6,512]{2,1,0:T(8,128)(2,1)S(1)} %get-tuple-element.42), channel_id=1, source_target_pairs={{0,31},{1,24},{2,25},{3,26},{4,27},{5,28},{6,29},{7,30},{8,7},{9,0... | collective-permute-start | bytes 55304 | tf_op jit(solution)/shard_map/ppermute | solution.py:136
  11.4 5.2 %collective-permute-start.10 = (bf16[3,6,512]{2,1,0:T(8,128)(2,1)S(1)}, bf16[3,6,512]{2,1,0:T(8,128)(2,1)S(1)}, u32[]{:S(2)}, u32[]{:S(2)}) collective-permute-start(bf16[3,6,512]{2,1,0:T(8,128)(2,1)S(1)} %get-tuple-element.43), channel_id=1, source_target_pairs={{0,24},{1,25},{2,26},{3,27},{4,28},{5,29},{6,30},{7,31},{8,0},{9,1... | collective-permute-start | bytes 55304 | tf_op jit(solution)/shard_map/ppermute | solution.py:136
  31.1 6.2 %collective-permute-start.5 = (bf16[3,6,512]{2,1,0:T(8,128)(2,1)S(1)}, bf16[3,6,512]{2,1,0:T(8,128)(2,1)S(1)}, u32[]{:S(2)}, u32[]{:S(2)}) collective-permute-start(bf16[3,6,512]{2,1,0:T(8,128)(2,1)S(1)} %slice.273), channel_id=1, source_target_pairs={{0,31},{1,24},{2,25},{3,26},{4,27},{5,28},{6,29},{7,30},{8,7},{9,0... | collective-permute-start | bytes 55304 | tf_op jit(solution)/shard_map/ppermute | solution.py:136
  82.5 18.5 %collective-permute-start.8 = (bf16[3,6,512]{2,1,0:T(8,128)(2,1)}, bf16[3,6,512]{2,1,0:T(8,128)(2,1)}, u32[]{:S(2)}, u32[]{:S(2)}) collective-permute-start(bf16[3,6,512]{2,1,0:T(8,128)(2,1)} %get-tuple-element.46), channel_id=1, source_target_pairs={{0,1},{1,2},{2,3},{3,4},{4,5},{5,6},{6,7},{7,0},{8,9},{9,10},{10,1... | collective-permute-start | bytes 55304 | tf_op jit(solution)/shard_map/ppermute | solution.py:136
  82.5 20.8 %collective-permute-start.7 = (bf16[3,6,512]{2,1,0:T(8,128)(2,1)}, bf16[3,6,512]{2,1,0:T(8,128)(2,1)}, u32[]{:S(2)}, u32[]{:S(2)}) collective-permute-start(bf16[3,6,512]{2,1,0:T(8,128)(2,1)} %get-tuple-element.47), channel_id=1, source_target_pairs={{0,8},{1,9},{2,10},{3,11},{4,12},{5,13},{6,14},{7,15},{8,16},{9,17... | collective-permute-start | bytes 55304 | tf_op jit(solution)/shard_map/ppermute | solution.py:136
  82.9 20.6 %collective-permute-start.6 = (bf16[3,6,512]{2,1,0:T(8,128)(2,1)}, bf16[3,6,512]{2,1,0:T(8,128)(2,1)}, u32[]{:S(2)}, u32[]{:S(2)}) collective-permute-start(bf16[3,6,512]{2,1,0:T(8,128)(2,1)} %get-tuple-element.44), channel_id=1, source_target_pairs={{0,9},{1,10},{2,11},{3,12},{4,13},{5,14},{6,15},{7,8},{8,17},{9,18... | collective-permute-start | bytes 55304 | tf_op jit(solution)/shard_map/ppermute | solution.py:136
  95.8 12.3 %collective-permute-start.14 = (bf16[9,6,512]{2,1,0:T(8,128)(2,1)}, bf16[9,6,512]{2,1,0:T(8,128)(2,1)S(1)}, u32[]{:S(2)}, u32[]{:S(2)}) collective-permute-start(bf16[9,6,512]{2,1,0:T(8,128)(2,1)} %slice.283), channel_id=1, source_target_pairs={{0,1},{1,2},{2,3},{3,4},{4,5},{5,6},{6,7},{7,0},{8,9},{9,10},{10,1... | collective-permute-start | bytes 165896 | tf_op jit(solution)/shard_map/ppermute | solution.py:136
  97.3 10.8 %collective-permute-start.13 = (bf16[3,18,512]{2,1,0:T(8,128)(2,1)}, bf16[3,18,512]{2,1,0:T(8,128)(2,1)S(1)}, u32[]{:S(2)}, u32[]{:S(2)}) collective-permute-start(bf16[3,18,512]{2,1,0:T(8,128)(2,1)} %slice.282), channel_id=1, source_target_pairs={{0,8},{1,9},{2,10},{3,11},{4,12},{5,13},{6,14},{7,15},{8,16},{9,17... | collective-permute-start | bytes 165896 | tf_op jit(solution)/shard_map/ppermute | solution.py:136
  101.0 7.1 %collective-permute-start.12 = (bf16[3,6,512]{2,1,0:T(8,128)(2,1)}, bf16[3,6,512]{2,1,0:T(8,128)(2,1)S(1)}, u32[]{:S(2)}, u32[]{:S(2)}) collective-permute-start(bf16[3,6,512]{2,1,0:T(8,128)(2,1)} %slice.281), channel_id=1, source_target_pairs={{0,9},{1,10},{2,11},{3,12},{4,13},{5,14},{6,15},{7,8},{8,17},{9,18... | collective-permute-start | bytes 55304 | tf_op jit(solution)/shard_map/ppermute | solution.py:136
  103.3 46.7 %collective-permute-start.28 = (bf16[16,128,512]{2,1,0:T(8,128)(2,1)}, bf16[16,128,512]{2,1,0:T(8,128)(2,1)}, u32[]{:S(2)}, u32[]{:S(2)}) collective-permute-start(bf16[16,128,512]{2,1,0:T(8,128)(2,1)} %dynamic-slice_bitcast_fusion), channel_id=1, source_target_pairs={{0,1},{1,0},{2,3},{3,2},{4,5},{5,4},{6,7},{7,6},{8,9},{9,8},{10,11... | collective-permute-start | bytes 6291464 | tf_op jit(solution)/shard_map/ppermute | solution.py:160
  139.9 8.1 %collective-permute-start.23 = (bf16[16,64,256]{2,1,0:T(8,128)(2,1)S(1)}, bf16[16,64,256]{2,1,0:T(8,128)(2,1)S(1)}, u32[]{:S(2)}, u32[]{:S(2)}) collective-permute-start(bf16[16,64,256]{2,1,0:T(8,128)(2,1)S(1)} %dynamic-slice_bitcast_fusion.3), channel_id=1, source_target_pairs={{0,1},{1,0},{2,3},{3,2},{4,5},{5,4},{6,7},{7,6},{8,9},{9,8},{10,11... | collective-permute-start | bytes 1572872 | tf_op jit(solution)/shard_map/ppermute | solution.py:160
  144.9 37.6 %collective-permute-start.17 = (bf16[9,6,512]{2,1,0:T(8,128)(2,1)S(1)}, bf16[9,6,512]{2,1,0:T(8,128)(2,1)S(1)}, u32[]{:S(2)}, u32[]{:S(2)}) collective-permute-start(bf16[9,6,512]{2,1,0:T(8,128)(2,1)S(1)} %slice.287), channel_id=1, source_target_pairs={{0,1},{1,2},{2,3},{3,4},{4,5},{5,6},{6,7},{7,0},{8,9},{9,10},{10,1... | collective-permute-start | bytes 165896 | tf_op jit(solution)/shard_map/ppermute | solution.py:136
  145.0 37.5 %collective-permute-start.16 = (bf16[3,18,512]{2,1,0:T(8,128)(2,1)S(1)}, bf16[3,18,512]{2,1,0:T(8,128)(2,1)S(1)}, u32[]{:S(2)}, u32[]{:S(2)}) collective-permute-start(bf16[3,18,512]{2,1,0:T(8,128)(2,1)S(1)} %slice.286), channel_id=1, source_target_pairs={{0,8},{1,9},{2,10},{3,11},{4,12},{5,13},{6,14},{7,15},{8,16},{9,17... | collective-permute-start | bytes 165896 | tf_op jit(solution)/shard_map/ppermute | solution.py:136
  148.0 34.5 %collective-permute-start.15 = (bf16[3,6,512]{2,1,0:T(8,128)(2,1)S(1)}, bf16[3,6,512]{2,1,0:T(8,128)(2,1)S(1)}, u32[]{:S(2)}, u32[]{:S(2)}) collective-permute-start(bf16[3,6,512]{2,1,0:T(8,128)(2,1)S(1)} %slice.285), channel_id=1, source_target_pairs={{0,9},{1,10},{2,11},{3,12},{4,13},{5,14},{6,15},{7,8},{8,17},{9,18... | collective-permute-start | bytes 55304 | tf_op jit(solution)/shard_map/ppermute | solution.py:136
  148.2 9.5 %collective-permute-start.24 = (bf16[8,64,256]{2,1,0:T(8,128)(2,1)S(1)}, bf16[8,64,256]{2,1,0:T(8,128)(2,1)S(1)}, u32[]{:S(2)}, u32[]{:S(2)}) collective-permute-start(bf16[8,64,256]{2,1,0:T(8,128)(2,1)S(1)} %dynamic-slice_bitcast_fusion.5), channel_id=1, source_target_pairs={{0,2},{1,3},{2,0},{3,1},{4,6},{5,7},{6,4},{7,5},{8,10},{9,11},{10,... | collective-permute-start | bytes 786440 | tf_op jit(solution)/shard_map/ppermute | solution.py:160
  152.3 27.5 %collective-permute-start.29 = (bf16[8,128,512]{2,1,0:T(8,128)(2,1)S(1)}, bf16[8,128,512]{2,1,0:T(8,128)(2,1)S(1)}, u32[]{:S(2)}, u32[]{:S(2)}) collective-permute-start(bf16[8,128,512]{2,1,0:T(8,128)(2,1)S(1)} %dynamic-slice_bitcast_fusion.1), channel_id=1, source_target_pairs={{0,2},{1,3},{2,0},{3,1},{4,6},{5,7},{6,4},{7,5},{8,10},{9,11},{10,... | collective-permute-start | bytes 3145736 | tf_op jit(solution)/shard_map/ppermute | solution.py:160
  157.8 5.0 %collective-permute-start.25 = (bf16[4,64,256]{2,1,0:T(8,128)(2,1)S(1)}, bf16[4,64,256]{2,1,0:T(8,128)(2,1)S(1)}, u32[]{:S(2)}, u32[]{:S(2)}) collective-permute-start(bf16[4,64,256]{2,1,0:T(8,128)(2,1)S(1)} %dynamic-slice_bitcast_fusion.6), channel_id=1, source_target_pairs={{0,4},{1,5},{2,6},{3,7},{4,0},{5,1},{6,2},{7,3},{8,12},{9,13},{10,... | collective-permute-start | bytes 393224 | tf_op jit(solution)/shard_map/ppermute | solution.py:160
  162.9 18.3 %collective-permute-start.26 = (bf16[2,64,256]{2,1,0:T(8,128)(2,1)S(1)}, bf16[2,64,256]{2,1,0:T(8,128)(2,1)S(1)}, u32[]{:S(2)}, u32[]{:S(2)}) collective-permute-start(bf16[2,64,256]{2,1,0:T(8,128)(2,1)S(1)} %dynamic-slice_bitcast_fusion.7), channel_id=1, source_target_pairs={{0,8},{8,0},{16,24},{24,16},{1,9},{9,1},{17,25},{25,17},{2,10},{10... | collective-permute-start | bytes 196616 | tf_op jit(solution)/shard_map/ppermute | solution.py:160
  180.2 13.7 %collective-permute-start.30 = (bf16[4,128,512]{2,1,0:T(8,128)(2,1)S(1)}, bf16[4,128,512]{2,1,0:T(8,128)(2,1)S(1)}, u32[]{:S(2)}, u32[]{:S(2)}) collective-permute-start(bf16[4,128,512]{2,1,0:T(8,128)(2,1)S(1)} %dynamic-slice_bitcast_fusion.2), channel_id=1, source_target_pairs={{0,4},{1,5},{2,6},{3,7},{4,0},{5,1},{6,2},{7,3},{8,12},{9,13},{10,... | collective-permute-start | bytes 1572872 | tf_op jit(solution)/shard_map/ppermute | solution.py:160
  181.2 5.1 %collective-permute-start.27 = (bf16[1,64,256]{2,1,0:T(8,128)(2,1)S(1)}, bf16[1,64,256]{2,1,0:T(8,128)(2,1)S(1)}, u32[]{:S(2)}, u32[]{:S(2)}) collective-permute-start(bf16[1,64,256]{2,1,0:T(8,128)(2,1)S(1)} %constant_dynamic-slice_fusion.1), channel_id=1, source_target_pairs={{0,16},{8,24},{16,0},{24,8},{1,17},{9,25},{17,1},{25,9},{2,18},{10... | collective-permute-start | bytes 98312 | tf_op jit(solution)/shard_map/ppermute | solution.py:160
  194.0 7.2 %collective-permute-start.31 = (bf16[2,128,512]{2,1,0:T(8,128)(2,1)S(1)}, bf16[2,128,512]{2,1,0:T(8,128)(2,1)S(1)}, u32[]{:S(2)}, u32[]{:S(2)}) collective-permute-start(bf16[2,128,512]{2,1,0:T(8,128)(2,1)S(1)} %dynamic-slice_bitcast_fusion.4), channel_id=1, source_target_pairs={{0,8},{8,0},{16,24},{24,16},{1,9},{9,1},{17,25},{25,17},{2,10},{10... | collective-permute-start | bytes 786440 | tf_op jit(solution)/shard_map/ppermute | solution.py:160
  201.3 7.3 %collective-permute-start.32 = (bf16[1,128,512]{2,1,0:T(8,128)(2,1)S(1)}, bf16[1,128,512]{2,1,0:T(8,128)(2,1)S(1)}, u32[]{:S(2)}, u32[]{:S(2)}) collective-permute-start(bf16[1,128,512]{2,1,0:T(8,128)(2,1)S(1)} %constant_dynamic-slice_fusion), channel_id=1, source_target_pairs={{0,16},{8,24},{16,0},{24,8},{1,17},{9,25},{17,1},{25,9},{2,18},{10... | collective-permute-start | bytes 393224 | tf_op jit(solution)/shard_map/ppermute | solution.py:160
  (75 other events, 393.0 us)

commit v2 on v1

v2 whole, which is shorter than its diff:
```python
import functools

import jax
import jax.numpy as jnp
import numpy as np
from jax import lax
from jax.experimental import pallas as pl
from jax.experimental.pallas import tpu as pltpu
from jax.sharding import PartitionSpec as P

HF = 4
HC = 8
WLAT = 6
WLON = 12
SLAT = 3
SLON = 6


EPSILON = 1e-05


VMEM = pl.BlockSpec(memory_space=pltpu.VMEM)
SMEM = pl.BlockSpec(memory_space=pltpu.SMEM)
F32 = jnp.float32
BF16 = jnp.bfloat16


def one_hot(sources, size):
    matrix = np.zeros((len(sources), size), np.float32)
    for row, source in enumerate(sources):
        if source >= 0:
            matrix[row, source] = 1.0
    return jnp.asarray(matrix, BF16)


def window_order(rows, cols):
    return [
        (a * WLAT + i, b * WLON + j)
        for a in range(rows // WLAT)
        for b in range(cols // WLON)
        for i in range(WLAT)
        for j in range(WLON)
    ]


def merge_order(rows, cols):
    return [
        (2 * a + low, 2 * b + side)
        for side in range(2)
        for low in range(2)
        for a, b in window_order(rows // 2, cols // 2)
    ]


def natural_order(rows, cols):
    return [(i, j) for i in range(rows) for j in range(cols)]


def roll_parts(rows, cols, ahead):
    if ahead:
        lat, lon = (range(SLAT), range(SLAT, rows)), (range(SLON), range(SLON, cols))
    else:
        lat = (range(rows - SLAT, rows), range(rows - SLAT))
        lon = (range(cols - SLON, cols), range(cols - SLON))
    pick = ((lat[0], lon[1]), (lat[1], lon[0]), (lat[0], lon[0]))
    return [[(i, j) for i in r for j in c] for r, c in pick]


def roll_matrices(rows, cols, ahead, order):
    shift = 1 if ahead else -1
    parts = [{cell: k for k, cell in enumerate(p)} for p in roll_parts(rows, cols, ahead)]
    found = [[], [], [], []]
    for i, j in order:
        row, col = i + shift * SLAT, j + shift * SLON
        out_row, out_col = not 0 <= row < rows, not 0 <= col < cols
        cell = (row % rows, col % cols)
        which = {(0, 0): 0, (1, 0): 1, (0, 1): 2, (1, 1): 3}[(int(out_row), int(out_col))]
        for k in range(4):
            found[k].append((cell if k == 0 else parts[k - 1][cell]) if k == which else -1)
    return found, [len(p) for p in parts]


def assembling(rows, cols, ahead, order, stored):
    place = {cell: k for k, cell in enumerate(stored)}
    found, sizes = roll_matrices(rows, cols, ahead, order)
    own = [place[c] if c != -1 else -1 for c in found[0]]
    return [one_hot(own, rows * cols)] + [one_hot(f, n) for f, n in zip(found[1:], sizes)]


def sending(rows, cols, ahead, stored):
    place = {cell: k for k, cell in enumerate(stored)}
    return [
        one_hot([place[c] for c in part], rows * cols) for part in roll_parts(rows, cols, ahead)
    ]


def send_parts(parts, ahead):
    step = -1 if ahead else 1
    return [send(parts[0], step, 0), send(parts[1], 0, step), send(parts[2], step, step)]


def mm(left, right):
    return jnp.dot(left, right, preferred_element_type=F32)


def mm_t(left, right):
    return lax.dot_general(left, right, (((1,), (1,)), ((), ())), preferred_element_type=F32)


def t_mm(left, right):
    return lax.dot_general(left, right, (((0,), (0,)), ((), ())), preferred_element_type=F32)


def gathered(values, matrices):
    total = mm(matrices[0][...], values[0][...])
    for value, matrix in zip(values[1:], matrices[1:]):
        total = total + mm(matrix[...], value[...])
    return total


def norm_parts(values):
    center = jnp.mean(values, axis=-1, keepdims=True)
    shifted = values - center
    spread = jnp.mean(shifted * shifted, axis=-1, keepdims=True)
    rate = lax.rsqrt(spread + EPSILON)
    return shifted * rate, rate


def norm_back(grad, unit, rate, gains):
    scaled = grad * gains
    first = jnp.mean(scaled, axis=-1, keepdims=True)
    second = jnp.mean(scaled * unit, axis=-1, keepdims=True)
    return rate * (scaled - first - unit * second), jnp.sum(grad * unit, axis=0, keepdims=True)


def lane_halves(value, size):
    lane = lax.broadcasted_iota(jnp.int32, value.shape, 1)
    return [
        jnp.where((lane >= k * size) & (lane < (k + 1) * size), value, jnp.zeros_like(value))
        for k in range(value.shape[1] // size)
    ]


def stacked(value, size):
    return jnp.concatenate(lane_halves(value, size), axis=0).astype(BF16)


def unstacked(value, size):
    cells = value.shape[0] * size // value.shape[1]
    lane = lax.broadcasted_iota(jnp.int32, (cells, value.shape[1]), 1)
    total = value[:cells]
    for k in range(1, value.shape[1] // size):
        total = jnp.where(lane >= k * size, value[k * cells : (k + 1) * cells], total)
    return total


def weights_of(query, keys, border, size):
    cells = keys.shape[0]
    scores = mm_t(query, keys) * size ** (-0.5)
    row = lax.broadcasted_iota(jnp.int32, scores.shape, 0)
    other = lax.broadcasted_iota(jnp.int32, scores.shape, 1)
    for _ in range(query.shape[0] // cells - 1):
        row = jnp.where(row >= cells, row - cells, row)
    allowed = (row >= border).astype(jnp.int32) == (other >= border).astype(jnp.int32)
    scores = jnp.where(allowed, scores, -1000000000.0)
    exponent = jnp.exp(scores - jnp.max(scores, axis=-1, keepdims=True))
    return exponent * (1.0 / jnp.sum(exponent, axis=-1, keepdims=True)), allowed


def attention_groups(cells, heads, inner, windows_lon):
    size = inner // heads
    lanes = 128 if inner % 128 == 0 and 128 % size == 0 else inner
    count = WLAT * WLON
    for window in range(cells // count):
        for start in range(0, inner, lanes):
            rows = slice(window * count, (window + 1) * count)
            yield window // windows_lon, rows, start, lanes, size


def border_of(edge, window_row):
    return (edge - window_row * WLAT) * WLON


def attend(packed, mixed_ref, edge, heads, windows_lon):
    inner = packed.shape[1] // 3
    for w, rows, start, lanes, size in attention_groups(
        packed.shape[0], heads, inner, windows_lon
    ):
        query = stacked(packed[rows, start : start + lanes], size)
        keys = packed[rows, inner + start : inner + start + lanes].astype(BF16)
        vals = packed[rows, 2 * inner + start : 2 * inner + start + lanes].astype(BF16)
        weights, _ = weights_of(query, keys, border_of(edge, w), size)
        mixed_ref[rows, start : start + lanes] = unstacked(mm(weights.astype(BF16), vals), size)


def attend_back(packed, grad_mixed, grad_ref, edge, heads, windows_lon):
    inner = packed.shape[1] // 3
    for w, rows, start, lanes, size in attention_groups(
        packed.shape[0], heads, inner, windows_lon
    ):
        query = stacked(packed[rows, start : start + lanes], size)
        keys = packed[rows, inner + start : inner + start + lanes].astype(BF16)
        vals = packed[rows, 2 * inner + start : 2 * inner + start + lanes].astype(BF16)
        grad = stacked(grad_mixed[rows, start : start + lanes], size)
        weights, allowed = weights_of(query, keys, border_of(edge, w), size)
        grad_weights = mm_t(grad, vals).astype(BF16).astype(F32)
        grad_vals = t_mm(weights.astype(BF16), grad)
        along = jnp.sum(grad_weights * weights, axis=-1, keepdims=True)
        slope = jnp.where(allowed, weights * (grad_weights - along), 0.0) * size ** (-0.5)
        slope = slope.astype(BF16)
        grad_ref[rows, start : start + lanes] = unstacked(mm(slope, keys), size)
        grad_ref[rows, inner + start : inner + start + lanes] = t_mm(slope, query)
        grad_ref[rows, 2 * inner + start : 2 * inner + start + lanes] = grad_vals


def rounded(value):
    return value.astype(BF16).astype(F32)


def fine_forward_kernel(windows_lon, *refs):
    (edge, own, p0, p1, p2, m0, m1, m2, m3, s1, s2, s3, gains, w_qkv, w_proj) = refs[:15]
    (rolled_ref, packed_ref, mixed_ref, result_ref, o1, o2, o3, mixed) = refs[15:]
    rolled = gathered((own, p0, p1, p2), (m0, m1, m2, m3))
    rolled_ref[...] = rolled.astype(BF16)
    unit, _ = norm_parts(rolled)
    packed = rounded(mm((unit * gains[...]).astype(BF16), w_qkv[...]))
    packed_ref[...] = packed.astype(BF16)
    attend(packed, mixed, edge[0], HF, windows_lon)
    blend = mixed[...].astype(BF16)
    mixed_ref[...] = blend
    result = (rolled + mm(blend, w_proj[...])).astype(BF16)
    result_ref[...] = result
    for out, pick in ((o1, s1), (o2, s2), (o3, s3)):
        out[...] = mm(pick[...], result).astype(BF16)


def coarse_kernel(windows_lon, *refs):
    (edge, own, p0, p1, p2, m0, m1, m2, m3, own_c, c0, c1, c2, n0, n1, n2, n3) = refs[:17]
    (s1, s2, s3, merge_gain, w_merge, gains, w_qkv, w_proj) = refs[17:25]
    (result_ref, out_ref, o1, o2, o3, g_merge_gain, g_merge, g_gain, g_qkv, g_proj) = refs[25:35]
    mixed, grad_packed_ref = refs[35:]
    fine = gathered((own, p0, p1, p2), (m0, m1, m2, m3))
    cells = fine.shape[0] // 4
    grid = jnp.concatenate([fine[k * cells : (k + 1) * cells] for k in range(4)], axis=1)
    merge_unit, merge_rate = norm_parts(grid)
    merge_normed = (merge_unit * merge_gain[...]).astype(BF16)
    rolled = rounded(mm(merge_normed, w_merge[...]))
    unit, rate = norm_parts(rolled)
    normed = (unit * gains[...]).astype(BF16)
    packed = rounded(mm(normed, w_qkv[...]))
    attend(packed, mixed, edge[0], HC, windows_lon)
    blend = mixed[...].astype(BF16)
    result_ref[...] = (rolled + mm(blend, w_proj[...])).astype(BF16)
    grad_out = gathered((own_c, c0, c1, c2), (n0, n1, n2, n3))
    grad_out_low = grad_out.astype(BF16)
    g_proj[...] = t_mm(blend, grad_out_low).astype(BF16)
    grad_mixed = rounded(mm_t(grad_out_low, w_proj[...]))
    attend_back(packed, grad_mixed, grad_packed_ref, edge[0], HC, windows_lon)
    grad_packed = grad_packed_ref[...].astype(BF16)
    grad_normed = rounded(mm_t(grad_packed, w_qkv[...]))
    g_qkv[...] = t_mm(normed, grad_packed).astype(BF16)
    grad_in, gain_sum = norm_back(grad_normed, unit, rate, gains[...])
    g_gain[...] = gain_sum
    grad_rolled = (grad_out + grad_in).astype(BF16)
    grad_merge = rounded(mm_t(grad_rolled, w_merge[...]))
    g_merge[...] = t_mm(merge_normed, grad_rolled).astype(BF16)
    grad_grid, gain_sum = norm_back(grad_merge, merge_unit, merge_rate, merge_gain[...])
    g_merge_gain[...] = gain_sum
    breadth = fine.shape[1]
    parts = [grad_grid[:, k * breadth : (k + 1) * breadth] for k in range(4)]
    out = jnp.concatenate(parts, axis=0).astype(BF16)
    out_ref[...] = out
    for part, pick in ((o1, s1), (o2, s2), (o3, s3)):
        part[...] = mm(pick[...], out).astype(BF16)


def fine_backward_kernel(windows_lon, *refs):
    (edge, own, p0, p1, p2, m0, m1, m2, m3, s1, s2, s3) = refs[:12]
    (rolled_ref, packed_ref, mixed_ref, gains, w_qkv, w_proj) = refs[12:18]
    (out_ref, o1, o2, o3, g_gain, g_qkv, g_proj, grad_packed_ref) = refs[18:]
    grad_out = gathered((own, p0, p1, p2), (m0, m1, m2, m3))
    grad_out_low = grad_out.astype(BF16)
    g_proj[...] = t_mm(mixed_ref[...], grad_out_low).astype(BF16)
    grad_mixed = rounded(mm_t(grad_out_low, w_proj[...]))
    packed = packed_ref[...].astype(F32)
    attend_back(packed, grad_mixed, grad_packed_ref, edge[0], HF, windows_lon)
    grad_packed = grad_packed_ref[...].astype(BF16)
    grad_normed = rounded(mm_t(grad_packed, w_qkv[...]))
    unit, rate = norm_parts(rolled_ref[...].astype(F32))
    g_qkv[...] = t_mm((unit * gains[...]).astype(BF16), grad_packed).astype(BF16)
    grad_in, gain_sum = norm_back(grad_normed, unit, rate, gains[...])
    g_gain[...] = gain_sum
    grad_rolled = (grad_out + grad_in).astype(BF16)
    out_ref[...] = grad_rolled
    for part, pick in ((o1, s1), (o2, s2), (o3, s3)):
        part[...] = mm(pick[...], grad_rolled).astype(BF16)


def roll_kernel(own, p0, p1, p2, m0, m1, m2, m3, out):
    out[...] = gathered((own, p0, p1, p2), (m0, m1, m2, m3)).astype(BF16)


def call(body, name, operands, outs, scratch=(), scalar=False, flops=0):
    shapes = [jax.ShapeDtypeStruct(shape, dtype) for shape, dtype in outs]
    moved = sum(v.size * v.dtype.itemsize for v in operands)
    moved += sum(v.size * v.dtype.itemsize for v in shapes)
    return pl.pallas_call(
        body,
        name=name,
        out_shape=shapes,
        in_specs=[SMEM if scalar and k == 0 else VMEM for k in range(len(operands))],
        out_specs=[VMEM] * len(shapes),
        scratch_shapes=[pltpu.VMEM(shape, F32) for shape in scratch],
        compiler_params=pltpu.CompilerParams(vmem_limit_bytes=56 * 1024 * 1024),
        cost_estimate=pl.CostEstimate(flops=flops, bytes_accessed=moved, transcendentals=0),
    )(*operands)


def cut_parts(grid, ahead):
    if ahead:
        lat, lon = (slice(None, SLAT), slice(SLAT, None)), (slice(None, SLON), slice(SLON, None))
    else:
        lat = (slice(-SLAT, None), slice(None, -SLAT))
        lon = (slice(-SLON, None), slice(None, -SLON))
    picks = ((lat[0], lon[1]), (lat[1], lon[0]), (lat[0], lon[0]))
    return [grid[r, c].reshape(-1, grid.shape[2]) for r, c in picks]


def shift_pairs(lat_step, lon_step):
    lats, lons = lax.axis_size("lat"), lax.axis_size("lon")
    return [
        (a * lons + b, ((a + lat_step) % lats) * lons + (b + lon_step) % lons)
        for a in range(lats)
        for b in range(lons)
    ]


def send(value, lat_step, lon_step):
    return lax.ppermute(value, ("lat", "lon"), shift_pairs(lat_step, lon_step))


def rotate_back(grid):
    above = send(grid[-SLAT:, :-SLON], 1, 0)
    beside = send(grid[:-SLAT, -SLON:], 0, 1)
    corner = send(grid[-SLAT:, -SLON:], 1, 1)
    low = jnp.concatenate([beside, grid[:-SLAT, :-SLON]], axis=1)
    return jnp.concatenate([jnp.concatenate([corner, above], axis=1), low], axis=0)


def halve(value, axis, step):
    count = lax.axis_size(axis)
    bit = (lax.axis_index(axis) // step) % 2
    kept = lax.dynamic_index_in_dim(value, bit, 1, keepdims=False)
    gone = lax.dynamic_index_in_dim(value, 1 - bit, 1, keepdims=False)
    came = lax.ppermute(gone, axis, [(i, i ^ step) for i in range(count)])
    return (kept.astype(jnp.float32) + came.astype(jnp.float32)).astype(value.dtype)


def reduce_pieces(value):
    lats, lons = lax.axis_size("lat"), lax.axis_size("lon")
    rows, columns = value.shape[1:]
    if lats & (lats - 1) or lons & (lons - 1):
        total = lax.psum_scatter(value, ("lat", "lon"), scatter_dimension=0, tiled=True)
        return total.reshape(rows, columns)
    step = 1
    while step < lons:
        left = lons // step
        value = value.reshape(lats * left // 2, 2, rows, columns)
        value = halve(value, "lon", step)
        step *= 2
    step = 1
    while step < lats:
        left = lats // step
        value = value.reshape(left // 2, 2, rows, columns)
        value = halve(value, "lat", step)
        step *= 2
    return value.reshape(rows, columns)


def as_pieces(value, devices, width):
    rows = value.shape[0] // devices
    value = value.astype(jnp.bfloat16).reshape(devices, rows, value.shape[1])
    parts = [value[:, :, i : i + width] for i in range(0, value.shape[2], width)]
    return jnp.concatenate(parts, axis=1)


def from_pieces(value, rows, columns):
    width = value.shape[1]
    parts = [value[i * rows : (i + 1) * rows] for i in range(columns // width)]
    return jnp.concatenate(parts, axis=1).astype(jnp.float32)


def local(
    tokens,
    fine_gain,
    fine_qkv,
    fine_proj,
    merge_gain,
    merge_weight,
    coarse_gain,
    coarse_qkv,
    coarse_proj,
    cotangent,
):
    fine_rows = tokens.shape[0]
    coarse_rows = fine_rows // 2
    lat_count = lax.axis_size("lat")
    lat_place = lax.axis_index("lat")
    fine_total = fine_rows * lat_count
    coarse_total = coarse_rows * lat_count
    fine_offset = lat_place * fine_rows
    coarse_offset = lat_place * coarse_rows
    grad_scale = (fine_total * tokens.shape[1] * lax.axis_size("lon") // 4) ** (-0.5)
    fine_cols, coarse_cols = tokens.shape[1], tokens.shape[1] // 2
    cells, breadth = fine_rows * fine_cols, tokens.shape[2]
    coarse_cells, coarse_breadth = cells // 4, coarse_proj.shape[1]
    fine = (fine_rows, fine_cols)
    coarse = (coarse_rows, coarse_cols)
    fine_edge = jnp.reshape(fine_total - SLAT - fine_offset, (1,)).astype(jnp.int32)
    coarse_edge = jnp.reshape(coarse_total - SLAT - coarse_offset, (1,)).astype(jnp.int32)
    sizes = [len(part) for part in roll_parts(*fine, True)]
    part_outs = [((n, breadth), BF16) for n in sizes]
    windowed, natural, merged = window_order(*fine), natural_order(*fine), merge_order(*fine)

    arrived = send_parts(cut_parts(tokens, True), True)
    cotangent_parts = send_parts(cut_parts(cotangent, True), True)
    inner = fine_proj.shape[0]
    rolled_fine, packed, blend, result, *parts = call(
        functools.partial(fine_forward_kernel, fine_cols // WLON),
        "fine_forward",
        [fine_edge, tokens.reshape(cells, breadth)]
        + arrived
        + assembling(*fine, True, windowed, natural)
        + sending(*fine, True, windowed)
        + [fine_gain[None], fine_qkv, fine_proj],
        [((cells, breadth), BF16), ((cells, 3 * inner), BF16), ((cells, inner), BF16)]
        + [((cells, breadth), BF16)]
        + part_outs,
        [(cells, inner)],
        True,
        3 * 10**9,
    )
    arrived = send_parts(parts, True)
    coarse_inner = coarse_proj.shape[0]
    coarse_windowed = window_order(*coarse)
    found = call(
        functools.partial(coarse_kernel, coarse_cols // WLON),
        "coarse",
        [coarse_edge, result]
        + arrived
        + assembling(*fine, True, merged, windowed)
        + [cotangent.reshape(coarse_cells, coarse_breadth)]
        + cotangent_parts
        + assembling(*coarse, True, coarse_windowed, natural_order(*coarse))
        + sending(*fine, False, merged)
        + [merge_gain[None], merge_weight, coarse_gain[None], coarse_qkv, coarse_proj],
        [((coarse_cells, coarse_breadth), BF16), ((cells, breadth), BF16)]
        + part_outs
        + [((1, 4 * breadth), F32), (merge_weight.shape, BF16), ((1, coarse_breadth), F32)]
        + [(coarse_qkv.shape, BF16), (coarse_proj.shape, BF16)],
        [(coarse_cells, coarse_inner), (coarse_cells, 3 * coarse_inner)],
        True,
        9 * 10**9,
    )
    coarse_result, grad_grid = found[:2]
    merge_gain_sum, merge_weight_sum, coarse_gain_sum = found[5][0], found[6], found[7][0]
    coarse_qkv_sum, coarse_proj_sum = found[8:]
    arrived = send_parts(found[2:5], False)
    grad_rolled, *parts = call(
        functools.partial(fine_backward_kernel, fine_cols // WLON),
        "fine_backward",
        [fine_edge, grad_grid]
        + arrived
        + assembling(*fine, False, windowed, merged)
        + sending(*fine, False, windowed)
        + [rolled_fine, packed, blend, fine_gain[None], fine_qkv, fine_proj],
        [((cells, breadth), BF16)]
        + part_outs
        + [((1, breadth), F32), (fine_qkv.shape, BF16), (fine_proj.shape, BF16)],
        [(cells, 3 * inner)],
        True,
        6 * 10**9,
    )
    fine_gain_sum, fine_qkv_sum, fine_proj_sum = parts[3][0], parts[4], parts[5]
    arrived = send_parts(parts[:3], False)
    (grad_tokens,) = call(
        roll_kernel,
        "final_roll",
        [grad_rolled] + arrived + assembling(*fine, False, natural, windowed),
        [((cells, breadth), BF16)],
        flops=10**8,
    )
    grad_tokens = grad_tokens.reshape(tokens.shape)
    coarse_grid = coarse_result.reshape(coarse_rows // WLAT, coarse_cols // WLON, WLAT, WLON, -1)
    coarse_grid = coarse_grid.transpose(0, 2, 1, 3, 4).reshape(cotangent.shape)
    output = rotate_back(coarse_grid)
    devices = lat_count * lax.axis_size("lon")

    def gather_sums(sums, width):
        pieces = [as_pieces(value, devices, width) for value in sums]
        total = reduce_pieces(jnp.concatenate(pieces, axis=1))
        found, start = [], 0
        for value, piece in zip(sums, pieces):
            part = total[start : start + piece.shape[1]]
            found.append(from_pieces(part, value.shape[0] // devices, value.shape[1]))
            start += piece.shape[1]
        return found

    merge_weight_sum, coarse_qkv_sum, coarse_proj_sum = gather_sums(
        (merge_weight_sum, coarse_qkv_sum, coarse_proj_sum), coarse_proj.shape[1]
    )
    fine_qkv_sum, fine_proj_sum = gather_sums((fine_qkv_sum, fine_proj_sum), 256)
    gains = [v.reshape(devices, -1) for v in (fine_gain_sum, merge_gain_sum, coarse_gain_sum)]
    gain_sums = reduce_pieces(jnp.concatenate(gains, axis=1)[:, None, :])[0]
    first, second = gains[0].shape[1], gains[0].shape[1] + gains[1].shape[1]
    fine_gain_sum, merge_gain_sum = gain_sums[:first], gain_sums[first:second]
    coarse_gain_sum = gain_sums[second:]
    return (
        output,
        grad_tokens,
        fine_gain_sum * grad_scale,
        fine_qkv_sum * grad_scale,
        fine_proj_sum * grad_scale,
        merge_gain_sum * grad_scale,
        merge_weight_sum * grad_scale,
        coarse_gain_sum * grad_scale,
        coarse_qkv_sum * grad_scale,
        coarse_proj_sum * grad_scale,
    )


def solution(mesh):
    return jax.shard_map(
        local,
        mesh=mesh,
        in_specs=(
            P("lat", "lon", None),
            P(),
            P(),
            P(),
            P(),
            P(),
            P(),
            P(),
            P(),
            P("lat", "lon", None),
        ),
        out_specs=(
            P("lat", "lon", None),
            P("lat", "lon", None),
            P(("lat", "lon")),
            P(("lat", "lon"), None),
            P(("lat", "lon"), None),
            P(("lat", "lon")),
            P(("lat", "lon"), None),
            P(("lat", "lon")),
            P(("lat", "lon"), None),
            P(("lat", "lon"), None),
        ),
        check_vma=False,
    )
```

time: 212 us -> 148 us (0.70)
  local copies, waits for them, and re-layouts: 57.4 us -> 17.9 us
  matrix products: 30.6 us -> 0 us
  Pallas kernels: 0 us -> 25.4 us
  other arithmetic: 25 us -> 9.34 us
  waiting for transfers between devices: 64.8 us -> 51.7 us
  starting transfers between devices: 30.6 us -> 41.6 us
    dot_general x27 -> x0, matrix products: 30.6 us -> none  [the longest x6 4.99 us: window_attention(): jnp.einsum('abhqk,abhkd->abhqd', attn_weights.astype(jnp.float32), values...]
    pallas_call x0 -> x4, Pallas kernels: none -> 25.4 us  [call(): pl.pallas_call(body, name=name, out_shape=shapes, in_specs=[SMEM if scala...]
    ppermute x15, waiting for transfers between devices: 58.5 us -> 44.2 us  [halve(): came = lax.ppermute(gone, axis, [(i, i ^ step) for i in range(count)])]
    reshape x15 -> x7, local copies, waits for them, and re-layouts: 14.1 us -> 0.75 us  [the longest x1 0.65 us: local(): cotangent.reshape(coarse_cells, coarse_breadth)]
    reduce_sum x12 -> x0, other arithmetic: 7.23 us -> none  [the longest x3 3.31 us: layer_norm(): return shifted * lax.rsqrt(spread + EPSILON) * gains]
    ppermute x15, starting transfers between devices: 10.7 us -> 17.4 us  [halve(): came = lax.ppermute(gone, axis, [(i, i ^ step) for i in range(count)])]
    convert_element_type x5 -> x0, local copies, waits for them, and re-layouts: 6.47 us -> none  [the longest x3 4.27 us: merge_forward(): packed_grid.astype(jnp.float32)]
    slice x17 -> x4, local copies, waits for them, and re-layouts: 7.65 us -> 2.55 us  [cut_parts(): return [grid[r, c].reshape(-1, grid.shape[2]) for r, c in picks]]
  transfers between devices with their start and end apart: 33 -> 33, of which waited for: 14 -> 15; matrix products, arithmetic and copies ran while one was open for 24% -> 13% of each run, Pallas kernels for 0% -> 7%
where the time goes in v2:
time: 148 us; the launch traced here: 147 us
  waiting for transfers between devices  51.7 us (35%)
  starting transfers between devices  41.6 us (28%)
  Pallas kernels  25.4 us (17%)
  local copies, waits for them, and re-layouts  17.9 us (12%)
  other arithmetic  9.34 us (6%)
    ppermute x15, waiting for transfers between devices, halve(): came = lax.ppermute(gone, axis, [(i, i ^ step) for i in range(count)])  44.2 us
    pallas_call x4, Pallas kernels, call(): pl.pallas_call(body, name=name, out_shape=shapes, in_specs=[SMEM if scala...  25.4 us
    ppermute x18, starting transfers between devices, send(): return lax.ppermute(value, ('lat', 'lon'), shift_pairs(lat_step, lon_step))  24.3 us
    ppermute x15, starting transfers between devices, halve(): came = lax.ppermute(gone, axis, [(i, i ^ step) for i in range(count)])  17.4 us
    unnamed x54, local copies, waits for them, and re-layouts  9.46 us
    ppermute x18, waiting for transfers between devices, send(): return lax.ppermute(value, ('lat', 'lon'), shift_pairs(lat_step, lon_step))  7.42 us
  transfers between devices with their start and end apart: 33, of which 15 were waited for; matrix products, arithmetic and copies ran while one was open for 13% of the time, Pallas kernels for 7%

profile of v2, /device:TPU:0, one launch (start us, length us, event | category | flops | bytes accessed | tf_op | source)
XLA Modules:
  0.0 147.1 jit_solution(5976464147691740453)
XLA Ops:
  1.6 5.1 %collective-permute-start = (bf16[54,512]{1,0:T(8,128)(2,1)S(1)}, bf16[54,512]{1,0:T(8,128)(2,1)S(1)}, u32[]{:S(2)}, u32[]{:S(2)}) collective-permute-start(bf16[54,512]{1,0:T(8,128)(2,1)S(1)} %reshape.176), channel_id=1, source_target_pairs={{0,24},{1,25},{2,26},{3,27},{4,28},{5,29},{6,30},{7,31},{8,0},{9,1... | collective-permute-start | bytes 165896 | tf_op jit(solution)/shard_map/ppermute | solution.py:339
  10.9 2.4 %collective-permute-done.2.refs_4_ = bf16[18,512]{1,0:T(8,128)(2,1)S(1)} collective-permute-done((bf16[18,512]{1,0:T(8,128)(2,1)S(1)}, bf16[18,512]{1,0:T(8,128)(2,1)S(1)}, u32[]{:S(2)}, u32[]{:S(2)}) %collective-permute-start.2) | collective-permute-done | bytes 18464 | tf_op jit(solution)/shard_map/ppermute | solution.py:339
  14.0 4.7 %fine_forward.1 = (bf16[288,512]{1,0:T(8,128)(2,1)}, bf16[288,768]{1,0:T(8,128)(2,1)}, bf16[288,256]{1,0:T(8,128)(2,1)}, bf16[288,512]{1,0:T(8,128)(2,1)}, bf16[...) custom-call(s32[1]{0:T(128)} %bitcast.1.refs_0_, bf16[288,512]{1,0:T(8,128)(2,1)} %bitcast.133, ...), custom_call_target="tpu_custom_call" | custom-call | flops 3000000000 | bytes 3094276 | tf_op jit(solution)/shard_map/fine_forward/pallas_call | solution.py:307
  18.7 2.2 %collective-permute-start.3 = (bf16[54,512]{1,0:T(8,128)(2,1)}, bf16[54,512]{1,0:T(8,128)(2,1)S(1)}, u32[]{:S(2)}, u32[]{:S(2)}) collective-permute-start(bf16[54,512]{1,0:T(8,128)(2,1)} %get-tuple-element.35), channel_id=1, source_target_pairs={{0,24},{1,25},{2,26},{3,27},{4,28},{5,29},{6,30},{7,31},{8,0},{9,1... | collective-permute-start | bytes 165896 | tf_op jit(solution)/shard_map/ppermute | solution.py:339
  20.9 2.5 %collective-permute-start.4 = (bf16[54,512]{1,0:T(8,128)(2,1)}, bf16[54,512]{1,0:T(8,128)(2,1)S(1)}, u32[]{:S(2)}, u32[]{:S(2)}) collective-permute-start(bf16[54,512]{1,0:T(8,128)(2,1)} %get-tuple-element.36), channel_id=1, source_target_pairs={{0,7},{1,0},{2,1},{3,2},{4,3},{5,4},{6,5},{7,6},{8,15},{9,8},{10,9... | collective-permute-start | bytes 165896 | tf_op jit(solution)/shard_map/ppermute | solution.py:339
  25.7 2.8 %collective-permute-start.5 = (bf16[18,512]{1,0:T(8,128)(2,1)}, bf16[18,512]{1,0:T(8,128)(2,1)S(1)}, u32[]{:S(2)}, u32[]{:S(2)}) collective-permute-start(bf16[18,512]{1,0:T(8,128)(2,1)} %get-tuple-element.37), channel_id=1, source_target_pairs={{0,31},{1,24},{2,25},{3,26},{4,27},{5,28},{6,29},{7,30},{8,7},{9,0... | collective-permute-start | bytes 55304 | tf_op jit(solution)/shard_map/ppermute | solution.py:339
  30.8 10.4 %coarse.1 = (bf16[72,512]{1,0:T(8,128)(2,1)}, bf16[288,512]{1,0:T(8,128)(2,1)}, bf16[54,512]{1,0:T(8,128)(2,1)}, bf16[54,512]{1,0:T(8,128)(2,1)}, bf16[18,512]{1...) custom-call(s32[1]{0:T(128)} %bitcast.refs_0_, ...), custom_call_target="tpu_custom_call" | custom-call | flops 8999999488 | bytes 9788900 | tf_op jit(solution)/shard_map/coarse/pallas_call | solution.py:307
  45.5 2.0 %copy-done = bf16[16,2,128,512]{3,2,1,0:T(8,128)(2,1)} copy-done((bf16[16,2,128,512]{3,2,1,0:T(8,128)(2,1)}, bf16[16,2,128,512]{3,2,1,0:T(8,128)(2,1)S(1)}, u32[]{:S(2)}) %copy-start) | copy-done | bytes 4194328
  52.6 7.9 %fine_backward.1 = (bf16[288,512]{1,0:T(8,128)(2,1)}, bf16[54,512]{1,0:T(8,128)(2,1)}, bf16[54,512]{1,0:T(8,128)(2,1)}, bf16[18,512]{1,0:T(8,128)(2,1)}, f32[1,5...) custom-call(s32[1]{0:T(128)} %bitcast.1.refs_0_, bf16[288,512]{1,0:T(8,128)(2,1)} %get-tuple-element.39.refs_1_, ...), custom_call_target="tpu_custom_call" | custom-call | flops 6000000000 | bytes 4144900 | tf_op jit(solution)/shard_map/fine_backward/pallas_call | solution.py:307
  69.3 2.0 %collective-permute-start.9 = (bf16[3,6,512]{2,1,0:T(8,128)(2,1)S(1)}, bf16[3,6,512]{2,1,0:T(8,128)(2,1)S(1)}, u32[]{:S(2)}, u32[]{:S(2)}) collective-permute-start(bf16[3,6,512]{2,1,0:T(8,128)(2,1)S(1)} %get-tuple-element.64), channel_id=1, source_target_pairs={{0,9},{1,10},{2,11},{3,12},{4,13},{5,14},{6,15},{7,8},{8,17},{9,18... | collective-permute-start | bytes 55304 | tf_op jit(solution)/shard_map/ppermute | solution.py:339
  71.3 1.8 %collective-permute-start.11 = (bf16[3,6,512]{2,1,0:T(8,128)(2,1)S(1)}, bf16[3,6,512]{2,1,0:T(8,128)(2,1)S(1)}, u32[]{:S(2)}, u32[]{:S(2)}) collective-permute-start(bf16[3,6,512]{2,1,0:T(8,128)(2,1)S(1)} %get-tuple-element.66), channel_id=1, source_target_pairs={{0,1},{1,2},{2,3},{3,4},{4,5},{5,6},{6,7},{7,0},{8,9},{9,10},{10,1... | collective-permute-start | bytes 55304 | tf_op jit(solution)/shard_map/ppermute | solution.py:339
  73.1 2.0 %collective-permute-start.10 = (bf16[3,6,512]{2,1,0:T(8,128)(2,1)S(1)}, bf16[3,6,512]{2,1,0:T(8,128)(2,1)S(1)}, u32[]{:S(2)}, u32[]{:S(2)}) collective-permute-start(bf16[3,6,512]{2,1,0:T(8,128)(2,1)S(1)} %get-tuple-element.67), channel_id=1, source_target_pairs={{0,8},{1,9},{2,10},{3,11},{4,12},{5,13},{6,14},{7,15},{8,16},{9,17... | collective-permute-start | bytes 55304 | tf_op jit(solution)/shard_map/ppermute | solution.py:339
  81.6 3.0 %collective-permute-done.21 = f32[2,1,96]{2,1,0:T(1,128)S(1)} collective-permute-done((f32[2,1,96]{2,1,0:T(1,128)S(1)}, f32[2,1,96]{2,1,0:T(1,128)S(1)}, u32[]{:S(2)}, u32[]{:S(2)}) %collective-permute-start.21) | collective-permute-done | bytes 800 | tf_op jit(solution)/shard_map/ppermute | solution.py:355
  84.6 2.7 %collective-permute-start.24 = (bf16[8,64,256]{2,1,0:T(8,128)(2,1)S(1)}, bf16[8,64,256]{2,1,0:T(8,128)(2,1)S(1)}, u32[]{:S(2)}, u32[]{:S(2)}) collective-permute-start(bf16[8,64,256]{2,1,0:T(8,128)(2,1)S(1)} %dynamic-slice_bitcast_fusion.5), channel_id=1, source_target_pairs={{0,2},{1,3},{2,0},{3,1},{4,6},{5,7},{6,4},{7,5},{8,10},{9,11},{10,... | collective-permute-start | bytes 786440 | tf_op jit(solution)/shard_map/ppermute | solution.py:355
  87.3 5.5 %collective-permute-done.24 = bf16[8,64,256]{2,1,0:T(8,128)(2,1)S(1)} collective-permute-done((bf16[8,64,256]{2,1,0:T(8,128)(2,1)S(1)}, bf16[8,64,256]{2,1,0:T(8,128)(2,1)S(1)}, u32[]{:S(2)}, u32[]{:S(2)}) %collective-permute-start.24) | collective-permute-done | bytes 262176 | tf_op jit(solution)/shard_map/ppermute | solution.py:355
  92.8 2.5 %collective-permute-start.22 = (f32[1,1,96]{2,1,0:T(1,128)S(1)}, f32[1,1,96]{2,1,0:T(1,128)S(1)}, u32[]{:S(2)}, u32[]{:S(2)}) collective-permute-start(f32[1,1,96]{2,1,0:T(1,128)S(1)} %constant_dynamic-slice_fusion.2), channel_id=1, source_target_pairs={{0,16},{8,24},{16,0},{24,8},{1,17},{9,25},{17,1},{25,9},{2,18},{10... | collective-permute-start | bytes 1160 | tf_op jit(solution)/shard_map/ppermute | solution.py:355
  98.3 4.8 %collective-permute-done.25 = bf16[4,64,256]{2,1,0:T(8,128)(2,1)S(1)} collective-permute-done((bf16[4,64,256]{2,1,0:T(8,128)(2,1)S(1)}, bf16[4,64,256]{2,1,0:T(8,128)(2,1)S(1)}, u32[]{:S(2)}, u32[]{:S(2)}) %collective-permute-start.25) | collective-permute-done | bytes 131104 | tf_op jit(solution)/shard_map/ppermute | solution.py:355
  104.9 2.6 %collective-permute-done.26 = bf16[2,64,256]{2,1,0:T(8,128)(2,1)S(1)} collective-permute-done((bf16[2,64,256]{2,1,0:T(8,128)(2,1)S(1)}, bf16[2,64,256]{2,1,0:T(8,128)(2,1)S(1)}, u32[]{:S(2)}, u32[]{:S(2)}) %collective-permute-start.26) | collective-permute-done | bytes 65568 | tf_op jit(solution)/shard_map/ppermute | solution.py:355
  107.5 11.8 %collective-permute-done.29 = bf16[8,128,512]{2,1,0:T(8,128)(2,1)S(1)} collective-permute-done((bf16[8,128,512]{2,1,0:T(8,128)(2,1)S(1)}, bf16[8,128,512]{2,1,0:T(8,128)(2,1)S(1)}, u32[]{:S(2)}, u32[]{:S(2)}) %collective-permute-start.29) | collective-permute-done | bytes 1048608 | tf_op jit(solution)/shard_map/ppermute | solution.py:355
  122.3 2.5 %final_roll.1 = bf16[288,512]{1,0:T(8,128)(2,1)} custom-call(bf16[288,512]{1,0:T(8,128)(2,1)} %get-tuple-element.46.own, bf16[54,512]{1,0:T(8,128)(2,1)} %copy-done.6, bf16[54,512]{1,0:T(8,128)(2,1)} %copy-done.7, bf16[18,512]{1,0:T(8,128)(2,1)} %copy-done.8, bf16[288,288]{1,0:T(8,128)(2,1)} %constant.315.clone.m0, bf16[288,54]{1,0:T(8,128)(2,1)} %constant.316.clone.m1, ...), custom_call_target="tpu_custom_call" | custom-call | flops 100000000 | bytes 957312 | tf_op jit(solution)/shard_map/final_roll/pallas_call | solution.py:307
  125.0 5.7 %collective-permute-done.30 = bf16[4,128,512]{2,1,0:T(8,128)(2,1)S(1)} collective-permute-done((bf16[4,128,512]{2,1,0:T(8,128)(2,1)S(1)}, bf16[4,128,512]{2,1,0:T(8,128)(2,1)S(1)}, u32[]{:S(2)}, u32[]{:S(2)}) %collective-permute-start.30) | collective-permute-done | bytes 524320 | tf_op jit(solution)/shard_map/ppermute | solution.py:355
  130.9 2.6 %collective-permute-start.31 = (bf16[2,128,512]{2,1,0:T(8,128)(2,1)S(1)}, bf16[2,128,512]{2,1,0:T(8,128)(2,1)S(1)}, u32[]{:S(2)}, u32[]{:S(2)}) collective-permute-start(bf16[2,128,512]{2,1,0:T(8,128)(2,1)S(1)} %dynamic-slice_bitcast_fusion.4), channel_id=1, source_target_pairs={{0,8},{8,0},{16,24},{24,16},{1,9},{9,1},{17,25},{25,17},{2,10},{10... | collective-permute-start | bytes 786440 | tf_op jit(solution)/shard_map/ppermute | solution.py:355
  133.5 5.6 %collective-permute-done.31 = bf16[2,128,512]{2,1,0:T(8,128)(2,1)S(1)} collective-permute-done((bf16[2,128,512]{2,1,0:T(8,128)(2,1)S(1)}, bf16[2,128,512]{2,1,0:T(8,128)(2,1)S(1)}, u32[]{:S(2)}, u32[]{:S(2)}) %collective-permute-start.31) | collective-permute-done | bytes 262176 | tf_op jit(solution)/shard_map/ppermute | solution.py:355
  140.5 4.6 %collective-permute-done.32 = bf16[1,128,512]{2,1,0:T(8,128)(2,1)S(1)} collective-permute-done((bf16[1,128,512]{2,1,0:T(8,128)(2,1)S(1)}, bf16[1,128,512]{2,1,0:T(8,128)(2,1)S(1)}, u32[]{:S(2)}, u32[]{:S(2)}) %collective-permute-start.32) | collective-permute-done | bytes 131104 | tf_op jit(solution)/shard_map/ppermute | solution.py:355
  (165 shorter events, 46.2 us)
Async XLA Ops:
  1.6 11.8 %collective-permute-start = (bf16[54,512]{1,0:T(8,128)(2,1)S(1)}, bf16[54,512]{1,0:T(8,128)(2,1)S(1)}, u32[]{:S(2)}, u32[]{:S(2)}) collective-permute-start(bf16[54,512]{1,0:T(8,128)(2,1)S(1)} %reshape.176), channel_id=1, source_target_pairs={{0,24},{1,25},{2,26},{3,27},{4,28},{5,29},{6,30},{7,31},{8,0},{9,1... | collective-permute-start | bytes 165896 | tf_op jit(solution)/shard_map/ppermute | solution.py:339
  7.6 5.7 %collective-permute-start.1 = (bf16[54,512]{1,0:T(8,128)(2,1)S(1)}, bf16[54,512]{1,0:T(8,128)(2,1)S(1)}, u32[]{:S(2)}, u32[]{:S(2)}) collective-permute-start(bf16[54,512]{1,0:T(8,128)(2,1)S(1)} %reshape.177), channel_id=1, source_target_pairs={{0,7},{1,0},{2,1},{3,2},{4,3},{5,4},{6,5},{7,6},{8,15},{9,8},{10,9... | collective-permute-start | bytes 165896 | tf_op jit(solution)/shard_map/ppermute | solution.py:339
  18.7 11.5 %collective-permute-start.3 = (bf16[54,512]{1,0:T(8,128)(2,1)}, bf16[54,512]{1,0:T(8,128)(2,1)S(1)}, u32[]{:S(2)}, u32[]{:S(2)}) collective-permute-start(bf16[54,512]{1,0:T(8,128)(2,1)} %get-tuple-element.35), channel_id=1, source_target_pairs={{0,24},{1,25},{2,26},{3,27},{4,28},{5,29},{6,30},{7,31},{8,0},{9,1... | collective-permute-start | bytes 165896 | tf_op jit(solution)/shard_map/ppermute | solution.py:339
  20.9 9.3 %collective-permute-start.4 = (bf16[54,512]{1,0:T(8,128)(2,1)}, bf16[54,512]{1,0:T(8,128)(2,1)S(1)}, u32[]{:S(2)}, u32[]{:S(2)}) collective-permute-start(bf16[54,512]{1,0:T(8,128)(2,1)} %get-tuple-element.36), channel_id=1, source_target_pairs={{0,7},{1,0},{2,1},{3,2},{4,3},{5,4},{6,5},{7,6},{8,15},{9,8},{10,9... | collective-permute-start | bytes 165896 | tf_op jit(solution)/shard_map/ppermute | solution.py:339
  23.5 5.6 %collective-permute-start.6 = (bf16[18,512]{1,0:T(8,128)(2,1)S(1)}, bf16[18,512]{1,0:T(8,128)(2,1)S(1)}, u32[]{:S(2)}, u32[]{:S(2)}) collective-permute-start(bf16[18,512]{1,0:T(8,128)(2,1)S(1)} %reshape.180), channel_id=1, source_target_pairs={{0,24},{1,25},{2,26},{3,27},{4,28},{5,29},{6,30},{7,31},{8,0},{9,1... | collective-permute-start | bytes 55304 | tf_op jit(solution)/shard_map/ppermute | solution.py:339
  41.2 10.7 %collective-permute-start.14 = (bf16[18,512]{1,0:T(8,128)(2,1)}, bf16[18,512]{1,0:T(8,128)(2,1)S(1)}, u32[]{:S(2)}, u32[]{:S(2)}) collective-permute-start(bf16[18,512]{1,0:T(8,128)(2,1)} %get-tuple-element.42), channel_id=1, source_target_pairs={{0,9},{1,10},{2,11},{3,12},{4,13},{5,14},{6,15},{7,8},{8,17},{9,18... | collective-permute-start | bytes 55304 | tf_op jit(solution)/shard_map/ppermute | solution.py:339
  41.3 10.7 %collective-permute-start.12 = (bf16[54,512]{1,0:T(8,128)(2,1)}, bf16[54,512]{1,0:T(8,128)(2,1)S(1)}, u32[]{:S(2)}, u32[]{:S(2)}) collective-permute-start(bf16[54,512]{1,0:T(8,128)(2,1)} %get-tuple-element.40), channel_id=1, source_target_pairs={{0,8},{1,9},{2,10},{3,11},{4,12},{5,13},{6,14},{7,15},{8,16},{9,17... | collective-permute-start | bytes 165896 | tf_op jit(solution)/shard_map/ppermute | solution.py:339
  42.9 9.1 %collective-permute-start.13 = (bf16[54,512]{1,0:T(8,128)(2,1)}, bf16[54,512]{1,0:T(8,128)(2,1)S(1)}, u32[]{:S(2)}, u32[]{:S(2)}) collective-permute-start(bf16[54,512]{1,0:T(8,128)(2,1)} %get-tuple-element.41), channel_id=1, source_target_pairs={{0,1},{1,2},{2,3},{3,4},{4,5},{5,6},{6,7},{7,0},{8,9},{9,10},{10,1... | collective-permute-start | bytes 165896 | tf_op jit(solution)/shard_map/ppermute | solution.py:339
  51.1 44.3 %collective-permute-start.28 = (bf16[16,128,512]{2,1,0:T(8,128)(2,1)}, bf16[16,128,512]{2,1,0:T(8,128)(2,1)S(1)}, u32[]{:S(2)}, u32[]{:S(2)}) collective-permute-start(bf16[16,128,512]{2,1,0:T(8,128)(2,1)} %dynamic-slice_bitcast_fusion), channel_id=1, source_target_pairs={{0,1},{1,0},{2,3},{3,2},{4,5},{5,4},{6,7},{7,6},{8,9},{9,8},{10,11... | collective-permute-start | bytes 6291464 | tf_op jit(solution)/shard_map/ppermute | solution.py:355
  62.1 5.8 %collective-permute-start.18 = (f32[16,1,96]{2,0,1:T(8,128)S(1)}, f32[16,1,96]{2,0,1:T(8,128)S(1)}, u32[]{:S(2)}, u32[]{:S(2)}) collective-permute-start(f32[16,1,96]{2,0,1:T(8,128)S(1)} %bitcast.141), channel_id=1, source_target_pairs={{0,1},{1,0},{2,3},{3,2},{4,5},{5,4},{6,7},{7,6},{8,9},{9,8},{10,11... | collective-permute-start | bytes 18440 | tf_op jit(solution)/shard_map/ppermute | solution.py:355
  67.2 13.7 %collective-permute-start.23 = (bf16[16,64,256]{2,1,0:T(8,128)(2,1)S(1)}, bf16[16,64,256]{2,1,0:T(8,128)(2,1)S(1)}, u32[]{:S(2)}, u32[]{:S(2)}) collective-permute-start(bf16[16,64,256]{2,1,0:T(8,128)(2,1)S(1)} %dynamic-slice_bitcast_fusion.3), channel_id=1, source_target_pairs={{0,1},{1,0},{2,3},{3,2},{4,5},{5,4},{6,7},{7,6},{8,9},{9,8},{10,11... | collective-permute-start | bytes 1572872 | tf_op jit(solution)/shard_map/ppermute | solution.py:355
  67.9 5.2 %collective-permute-start.19 = (f32[8,1,96]{2,0,1:T(8,128)S(1)}, f32[8,1,96]{2,0,1:T(8,128)S(1)}, u32[]{:S(2)}, u32[]{:S(2)}) collective-permute-start(f32[8,1,96]{2,0,1:T(8,128)S(1)} %bitcast.142), channel_id=1, source_target_pairs={{0,2},{1,3},{2,0},{3,1},{4,6},{5,7},{6,4},{7,5},{8,10},{9,11},{10,... | collective-permute-start | bytes 9224 | tf_op jit(solution)/shard_map/ppermute | solution.py:355
  69.3 7.0 %collective-permute-start.9 = (bf16[3,6,512]{2,1,0:T(8,128)(2,1)S(1)}, bf16[3,6,512]{2,1,0:T(8,128)(2,1)S(1)}, u32[]{:S(2)}, u32[]{:S(2)}) collective-permute-start(bf16[3,6,512]{2,1,0:T(8,128)(2,1)S(1)} %get-tuple-element.64), channel_id=1, source_target_pairs={{0,9},{1,10},{2,11},{3,12},{4,13},{5,14},{6,15},{7,8},{8,17},{9,18... | collective-permute-start | bytes 55304 | tf_op jit(solution)/shard_map/ppermute | solution.py:339
  71.3 6.4 %collective-permute-start.11 = (bf16[3,6,512]{2,1,0:T(8,128)(2,1)S(1)}, bf16[3,6,512]{2,1,0:T(8,128)(2,1)S(1)}, u32[]{:S(2)}, u32[]{:S(2)}) collective-permute-start(bf16[3,6,512]{2,1,0:T(8,128)(2,1)S(1)} %get-tuple-element.66), channel_id=1, source_target_pairs={{0,1},{1,2},{2,3},{3,4},{4,5},{5,6},{6,7},{7,0},{8,9},{9,10},{10,1... | collective-permute-start | bytes 55304 | tf_op jit(solution)/shard_map/ppermute | solution.py:339
  73.1 5.6 %collective-permute-start.10 = (bf16[3,6,512]{2,1,0:T(8,128)(2,1)S(1)}, bf16[3,6,512]{2,1,0:T(8,128)(2,1)S(1)}, u32[]{:S(2)}, u32[]{:S(2)}) collective-permute-start(bf16[3,6,512]{2,1,0:T(8,128)(2,1)S(1)} %get-tuple-element.67), channel_id=1, source_target_pairs={{0,8},{1,9},{2,10},{3,11},{4,12},{5,13},{6,14},{7,15},{8,16},{9,17... | collective-permute-start | bytes 55304 | tf_op jit(solution)/shard_map/ppermute | solution.py:339
  79.4 42.2 %collective-permute-start.17 = (bf16[18,512]{1,0:T(8,128)(2,1)}, bf16[18,512]{1,0:T(8,128)(2,1)S(1)}, u32[]{:S(2)}, u32[]{:S(2)}) collective-permute-start(bf16[18,512]{1,0:T(8,128)(2,1)} %get-tuple-element.49), channel_id=1, source_target_pairs={{0,9},{1,10},{2,11},{3,12},{4,13},{5,14},{6,15},{7,8},{8,17},{9,18... | collective-permute-start | bytes 55304 | tf_op jit(solution)/shard_map/ppermute | solution.py:339
  79.4 42.2 %collective-permute-start.15 = (bf16[54,512]{1,0:T(8,128)(2,1)}, bf16[54,512]{1,0:T(8,128)(2,1)S(1)}, u32[]{:S(2)}, u32[]{:S(2)}) collective-permute-start(bf16[54,512]{1,0:T(8,128)(2,1)} %get-tuple-element.47), channel_id=1, source_target_pairs={{0,8},{1,9},{2,10},{3,11},{4,12},{5,13},{6,14},{7,15},{8,16},{9,17... | collective-permute-start | bytes 165896 | tf_op jit(solution)/shard_map/ppermute | solution.py:339
  79.9 41.7 %collective-permute-start.16 = (bf16[54,512]{1,0:T(8,128)(2,1)}, bf16[54,512]{1,0:T(8,128)(2,1)S(1)}, u32[]{:S(2)}, u32[]{:S(2)}) collective-permute-start(bf16[54,512]{1,0:T(8,128)(2,1)} %get-tuple-element.48), channel_id=1, source_target_pairs={{0,1},{1,2},{2,3},{3,4},{4,5},{5,6},{6,7},{7,0},{8,9},{9,10},{10,1... | collective-permute-start | bytes 165896 | tf_op jit(solution)/shard_map/ppermute | solution.py:339
  84.6 8.3 %collective-permute-start.24 = (bf16[8,64,256]{2,1,0:T(8,128)(2,1)S(1)}, bf16[8,64,256]{2,1,0:T(8,128)(2,1)S(1)}, u32[]{:S(2)}, u32[]{:S(2)}) collective-permute-start(bf16[8,64,256]{2,1,0:T(8,128)(2,1)S(1)} %dynamic-slice_bitcast_fusion.5), channel_id=1, source_target_pairs={{0,2},{1,3},{2,0},{3,1},{4,6},{5,7},{6,4},{7,5},{8,10},{9,11},{10,... | collective-permute-start | bytes 786440 | tf_op jit(solution)/shard_map/ppermute | solution.py:355
  92.8 5.2 %collective-permute-start.22 = (f32[1,1,96]{2,1,0:T(1,128)S(1)}, f32[1,1,96]{2,1,0:T(1,128)S(1)}, u32[]{:S(2)}, u32[]{:S(2)}) collective-permute-start(f32[1,1,96]{2,1,0:T(1,128)S(1)} %constant_dynamic-slice_fusion.2), channel_id=1, source_target_pairs={{0,16},{8,24},{16,0},{24,8},{1,17},{9,25},{17,1},{25,9},{2,18},{10... | collective-permute-start | bytes 1160 | tf_op jit(solution)/shard_map/ppermute | solution.py:355
  96.2 23.1 %collective-permute-start.29 = (bf16[8,128,512]{2,1,0:T(8,128)(2,1)S(1)}, bf16[8,128,512]{2,1,0:T(8,128)(2,1)S(1)}, u32[]{:S(2)}, u32[]{:S(2)}) collective-permute-start(bf16[8,128,512]{2,1,0:T(8,128)(2,1)S(1)} %dynamic-slice_bitcast_fusion.1), channel_id=1, source_target_pairs={{0,2},{1,3},{2,0},{3,1},{4,6},{5,7},{6,4},{7,5},{8,10},{9,11},{10,... | collective-permute-start | bytes 3145736 | tf_op jit(solution)/shard_map/ppermute | solution.py:355
  119.7 11.0 %collective-permute-start.30 = (bf16[4,128,512]{2,1,0:T(8,128)(2,1)S(1)}, bf16[4,128,512]{2,1,0:T(8,128)(2,1)S(1)}, u32[]{:S(2)}, u32[]{:S(2)}) collective-permute-start(bf16[4,128,512]{2,1,0:T(8,128)(2,1)S(1)} %dynamic-slice_bitcast_fusion.2), channel_id=1, source_target_pairs={{0,4},{1,5},{2,6},{3,7},{4,0},{5,1},{6,2},{7,3},{8,12},{9,13},{10,... | collective-permute-start | bytes 1572872 | tf_op jit(solution)/shard_map/ppermute | solution.py:355
  130.9 8.2 %collective-permute-start.31 = (bf16[2,128,512]{2,1,0:T(8,128)(2,1)S(1)}, bf16[2,128,512]{2,1,0:T(8,128)(2,1)S(1)}, u32[]{:S(2)}, u32[]{:S(2)}) collective-permute-start(bf16[2,128,512]{2,1,0:T(8,128)(2,1)S(1)} %dynamic-slice_bitcast_fusion.4), channel_id=1, source_target_pairs={{0,8},{8,0},{16,24},{24,16},{1,9},{9,1},{17,25},{25,17},{2,10},{10... | collective-permute-start | bytes 786440 | tf_op jit(solution)/shard_map/ppermute | solution.py:355
  139.2 5.9 %collective-permute-start.32 = (bf16[1,128,512]{2,1,0:T(8,128)(2,1)S(1)}, bf16[1,128,512]{2,1,0:T(8,128)(2,1)S(1)}, u32[]{:S(2)}, u32[]{:S(2)}) collective-permute-start(bf16[1,128,512]{2,1,0:T(8,128)(2,1)S(1)} %constant_dynamic-slice_fusion), channel_id=1, source_target_pairs={{0,16},{8,24},{16,0},{24,8},{1,17},{9,25},{17,1},{25,9},{2,18},{10... | collective-permute-start | bytes 393224 | tf_op jit(solution)/shard_map/ppermute | solution.py:355
  (32 other events, 116.9 us)

commit v3 on v2

--- a/solution.py
+++ b/solution.py
@@ -347,34 +347,109 @@
     return jnp.concatenate([jnp.concatenate([corner, above], axis=1), low], axis=0)
 
 
-def halve(value, axis, step):
-    count = lax.axis_size(axis)
-    bit = (lax.axis_index(axis) // step) % 2
-    kept = lax.dynamic_index_in_dim(value, bit, 1, keepdims=False)
-    gone = lax.dynamic_index_in_dim(value, 1 - bit, 1, keepdims=False)
-    came = lax.ppermute(gone, axis, [(i, i ^ step) for i in range(count)])
-    return (kept.astype(jnp.float32) + came.astype(jnp.float32)).astype(value.dtype)
-
-
-def reduce_pieces(value):
+def hop_orders():
+    lons = [("lon", 1 << k) for k in range(lax.axis_size("lon").bit_length() - 1)]
+    lats = [("lat", 1 << k) for k in range(lax.axis_size("lat").bit_length() - 1)]
+    first, rest = lons[:1], lons[1:]
+    return (
+        first + rest + lats,
+        first + rest[::-1] + lats,
+        first + lats[:1] + rest + lats[1:],
+    )
+
+
+def sum_kernel(orders, *refs):
+    count = len(orders)
+    hops = len(orders[0])
+    sources, outs = refs[:count], refs[count : 2 * count]
+    lands = [refs[2 * count + c * hops : 2 * count + (c + 1) * hops] for c in range(count)]
+    send_sem, recv_sem = refs[2 * count + count * hops :]
+    place = {"lat": lax.axis_index("lat"), "lon": lax.axis_index("lon")}
+
+    def bit_of(axis, step):
+        return (place[axis] // step) % 2
+
+    def partner(axis, step):
+        where = dict(place)
+        where[axis] = place[axis] + step - 2 * step * bit_of(axis, step)
+        return (where["lat"], where["lon"])
+
+    barrier = pltpu.get_barrier_semaphore()
+    for axis, step in orders[0]:
+        pl.semaphore_signal(
+            barrier, inc=1, device_id=partner(axis, step), device_id_type=pl.DeviceIdType.MESH
+        )
+    pl.semaphore_wait(barrier, hops)
+
+    def begin(chunk, hop):
+        axis, step = orders[chunk][hop]
+        source = sources[chunk] if hop == 0 else lands[chunk][hop - 1]
+        half = source.shape[0] // 2
+        copy = pltpu.make_async_remote_copy(
+            src_ref=source.at[pl.ds((1 - bit_of(axis, step)) * half, half)],
+            dst_ref=lands[chunk][hop],
+            send_sem=send_sem.at[chunk, hop],
+            recv_sem=recv_sem.at[chunk, hop],
+            device_id=partner(axis, step),
+            device_id_type=pl.DeviceIdType.MESH,
+        )
+        copy.start()
+        return copy
+
+    flying = [begin(chunk, 0) for chunk in range(count)]
+    for hop in range(hops):
+        for chunk in range(count):
+            axis, step = orders[chunk][hop]
+            flying[chunk].wait()
+            source = sources[chunk] if hop == 0 else lands[chunk][hop - 1]
+            land = lands[chunk][hop]
+            half = land.shape[0]
+            start = bit_of(axis, step) * half
+            target = land if hop < hops - 1 else outs[chunk]
+
+            def add(piece, carry):
+                total = land[piece].astype(F32) + source[start + piece].astype(F32)
+                target[piece] = total.astype(target.dtype)
+                return carry
+
+            lax.fori_loop(0, half, add, 0)
+            if hop < hops - 1:
+                flying[chunk] = begin(chunk, hop + 1)
+
+
+def reduce_chunks(chunks):
     lats, lons = lax.axis_size("lat"), lax.axis_size("lon")
-    rows, columns = value.shape[1:]
-    if lats & (lats - 1) or lons & (lons - 1):
-        total = lax.psum_scatter(value, ("lat", "lon"), scatter_dimension=0, tiled=True)
-        return total.reshape(rows, columns)
-    step = 1
-    while step < lons:
-        left = lons // step
-        value = value.reshape(lats * left // 2, 2, rows, columns)
-        value = halve(value, "lon", step)
-        step *= 2
-    step = 1
-    while step < lats:
-        left = lats // step
-        value = value.reshape(left // 2, 2, rows, columns)
-        value = halve(value, "lat", step)
-        step *= 2
-    return value.reshape(rows, columns)
+    if lats & (lats - 1) or lons & (lons - 1) or lats < 2 or lons < 2:
+        return [
+            lax.psum_scatter(c, ("lat", "lon"), scatter_dimension=0, tiled=True)[0].astype(F32)
+            for c in chunks
+        ]
+    orders = hop_orders()[: len(chunks)]
+    hops = len(orders[0])
+    highest = [("lat", 1 << k) for k in reversed(range(lats.bit_length() - 1))]
+    highest += [("lon", 1 << k) for k in reversed(range(lons.bit_length() - 1))]
+    ready, lands, outs = [], [], []
+    for chunk, order in zip(chunks, orders):
+        tail = chunk.shape[1:]
+        moved = chunk.reshape([2] * hops + list(tail))
+        axes = [highest.index(bit) for bit in order] + [hops, hops + 1]
+        ready.append(moved.transpose(axes).reshape(chunk.shape))
+        lands += [pltpu.VMEM((1 << (hops - 1 - k),) + tail, BF16) for k in range(hops)]
+        outs.append(jax.ShapeDtypeStruct((1,) + tail, F32))
+    sums = pl.pallas_call(
+        functools.partial(sum_kernel, orders),
+        name="gradient_sums",
+        out_shape=outs,
+        in_specs=[VMEM] * len(ready),
+        out_specs=[VMEM] * len(ready),
+        scratch_shapes=lands
+        + [pltpu.SemaphoreType.DMA((len(ready), hops)), pltpu.SemaphoreType.DMA((len(ready), hops))],
+        compiler_params=pltpu.CompilerParams(
+            collective_id=0, has_side_effects=True, vmem_limit_bytes=40 * 1024 * 1024
+        ),
+        cost_estimate=pl.CostEstimate(flops=10**7, bytes_accessed=10**8, transcendentals=0),
+    )(*ready)
+    return [value[0] for value in sums]
 
 
 def as_pieces(value, devices, width):
@@ -496,25 +571,32 @@
     output = rotate_back(coarse_grid)
     devices = lat_count * lax.axis_size("lon")
 
-    def gather_sums(sums, width):
-        pieces = [as_pieces(value, devices, width) for value in sums]
-        total = reduce_pieces(jnp.concatenate(pieces, axis=1))
-        found, start = [], 0
-        for value, piece in zip(sums, pieces):
-            part = total[start : start + piece.shape[1]]
-            found.append(from_pieces(part, value.shape[0] // devices, value.shape[1]))
-            start += piece.shape[1]
-        return found
-
-    merge_weight_sum, coarse_qkv_sum, coarse_proj_sum = gather_sums(
-        (merge_weight_sum, coarse_qkv_sum, coarse_proj_sum), coarse_proj.shape[1]
-    )
-    fine_qkv_sum, fine_proj_sum = gather_sums((fine_qkv_sum, fine_proj_sum), 256)
-    gains = [v.reshape(devices, -1) for v in (fine_gain_sum, merge_gain_sum, coarse_gain_sum)]
-    gain_sums = reduce_pieces(jnp.concatenate(gains, axis=1)[:, None, :])[0]
-    first, second = gains[0].shape[1], gains[0].shape[1] + gains[1].shape[1]
+    gains = [v.reshape(devices, 1, -1) for v in (fine_gain_sum, merge_gain_sum, coarse_gain_sum)]
+    gain_rows = jnp.concatenate(gains, axis=2).astype(BF16)
+    gain_rows = jnp.pad(gain_rows, ((0, 0), (0, 15), (0, 256 - gain_rows.shape[2])))
+    width = merge_weight.shape[1]
+    mixed = [as_pieces(v, devices, 256) for v in (coarse_proj_sum, fine_qkv_sum, fine_proj_sum)]
+    heights = [v.shape[1] for v in mixed]
+    merge_weight_total, coarse_qkv_total, total = reduce_chunks(
+        [
+            as_pieces(merge_weight_sum, devices, width),
+            as_pieces(coarse_qkv_sum, devices, width),
+            jnp.concatenate(mixed + [gain_rows], axis=1),
+        ]
+    )
+    merge_weight_sum = merge_weight_total
+    coarse_qkv_sum = from_pieces(
+        coarse_qkv_total, coarse_qkv.shape[0] // devices, coarse_qkv.shape[1]
+    )
+    starts = [0, heights[0], heights[0] + heights[1], sum(heights)]
+    coarse_proj_sum, fine_qkv_sum, fine_proj_sum = [
+        from_pieces(total[starts[k] : starts[k + 1]], w.shape[0] // devices, w.shape[1])
+        for k, w in enumerate((coarse_proj, fine_qkv, fine_proj))
+    ]
+    first, second = gains[0].shape[2], gains[0].shape[2] + gains[1].shape[2]
+    gain_sums = total[starts[3]]
     fine_gain_sum, merge_gain_sum = gain_sums[:first], gain_sums[first:second]
-    coarse_gain_sum = gain_sums[second:]
+    coarse_gain_sum = gain_sums[second : second + gains[2].shape[2]]
     return (
         output,
         grad_tokens,

time: 148 us -> 130 us (0.88)
  Pallas kernels: 25.4 us -> 62.8 us
  waiting for transfers between devices: 51.7 us -> 15.2 us
  starting transfers between devices: 41.6 us -> 22.6 us
  local copies, waits for them, and re-layouts: 17.9 us -> 21.7 us
  other arithmetic: 9.34 us -> 6.03 us
    ppermute x15 -> x0, waiting for transfers between devices: 44.2 us -> none  [halve(): came = lax.ppermute(gone, axis, [(i, i ^ step) for i in range(count)])]
    pallas_call x0 -> x1, Pallas kernels: none -> 37.5 us  [reduce_chunks(): pl.pallas_call(functools.partial(sum_kernel, orders), name='gradient_sums...]
    ppermute x15 -> x0, starting transfers between devices: 17.4 us -> none  [halve(): came = lax.ppermute(gone, axis, [(i, i ^ step) for i in range(count)])]
    ppermute x18, waiting for transfers between devices: 7.42 us -> 15.2 us  [send(): return lax.ppermute(value, ('lat', 'lon'), shift_pairs(lat_step, lon_step))]
    transpose x0 -> x2, local copies, waits for them, and re-layouts: none -> 3.12 us  [reduce_chunks(): ready.append(moved.transpose(axes).reshape(chunk.shape))]
    unnamed x54 -> x61, local copies, waits for them, and re-layouts: 9.46 us -> 12.3 us
    pallas_call x3 -> x0, other arithmetic: 2.68 us -> none  [call(): pl.pallas_call(body, name=name, out_shape=shapes, in_specs=[SMEM if scala...]
    squeeze x12 -> x0, local copies, waits for them, and re-layouts: 1.84 us -> none  [halve(): gone = lax.dynamic_index_in_dim(value, 1 - bit, 1, keepdims=False)]
  transfers between devices with their start and end apart: 33 -> 18, of which waited for: 15 -> 5; matrix products, arithmetic and copies ran while one was open for 13% -> 9% of each run, Pallas kernels for 7% -> 0%
where the time goes in v3:
time: 130 us; the launch traced here: 129 us
  Pallas kernels  62.8 us (48%)
  starting transfers between devices  22.6 us (17%)
  local copies, waits for them, and re-layouts  21.7 us (17%)
  waiting for transfers between devices  15.2 us (12%)
  other arithmetic  6.03 us (5%)
    pallas_call x1, Pallas kernels, reduce_chunks(): pl.pallas_call(functools.partial(sum_kernel, orders), name='gradient_sums...  37.5 us
    pallas_call x4, Pallas kernels, call(): pl.pallas_call(body, name=name, out_shape=shapes, in_specs=[SMEM if scala...  25.4 us
    ppermute x18, starting transfers between devices, send(): return lax.ppermute(value, ('lat', 'lon'), shift_pairs(lat_step, lon_step))  22.6 us
    ppermute x18, waiting for transfers between devices, send(): return lax.ppermute(value, ('lat', 'lon'), shift_pairs(lat_step, lon_step))  15.2 us
    unnamed x61, local copies, waits for them, and re-layouts  12.3 us
    transpose x2, local copies, waits for them, and re-layouts, reduce_chunks(): ready.append(moved.transpose(axes).reshape(chunk.shape))  3.12 us
  transfers between devices with their start and end apart: 18, of which 5 were waited for; matrix products, arithmetic and copies ran while one was open for 9% of the time, Pallas kernels for 0%

profile of v3, /device:TPU:0, one launch (start us, length us, event | category | flops | bytes accessed | tf_op | source)
XLA Modules:
  0.0 129.3 jit_solution(4016875920450671625)
XLA Ops:
  1.6 5.1 %collective-permute-start = (bf16[54,512]{1,0:T(8,128)(2,1)S(1)}, bf16[54,512]{1,0:T(8,128)(2,1)S(1)}, u32[]{:S(2)}, u32[]{:S(2)}) collective-permute-start(bf16[54,512]{1,0:T(8,128)(2,1)S(1)} %reshape.164), channel_id=1, source_target_pairs={{0,24},{1,25},{2,26},{3,27},{4,28},{5,29},{6,30},{7,31},{8,0},{9,1... | collective-permute-start | bytes 165896 | tf_op jit(solution)/shard_map/ppermute | solution.py:339
  7.6 1.7 %collective-permute-start.1 = (bf16[54,512]{1,0:T(8,128)(2,1)S(1)}, bf16[54,512]{1,0:T(8,128)(2,1)S(1)}, u32[]{:S(2)}, u32[]{:S(2)}) collective-permute-start(bf16[54,512]{1,0:T(8,128)(2,1)S(1)} %reshape.165), channel_id=1, source_target_pairs={{0,7},{1,0},{2,1},{3,2},{4,3},{5,4},{6,5},{7,6},{8,15},{9,8},{10,9... | collective-permute-start | bytes 165896 | tf_op jit(solution)/shard_map/ppermute | solution.py:339
  10.9 2.4 %collective-permute-done.2.refs_4_ = bf16[18,512]{1,0:T(8,128)(2,1)S(1)} collective-permute-done((bf16[18,512]{1,0:T(8,128)(2,1)S(1)}, bf16[18,512]{1,0:T(8,128)(2,1)S(1)}, u32[]{:S(2)}, u32[]{:S(2)}) %collective-permute-start.2) | collective-permute-done | bytes 18464 | tf_op jit(solution)/shard_map/ppermute | solution.py:339
  14.0 4.7 %fine_forward.1 = (bf16[288,512]{1,0:T(8,128)(2,1)}, bf16[288,768]{1,0:T(8,128)(2,1)}, bf16[288,256]{1,0:T(8,128)(2,1)}, bf16[288,512]{1,0:T(8,128)(2,1)}, bf16[...) custom-call(s32[1]{0:T(128)} %bitcast.1.refs_0_, bf16[288,512]{1,0:T(8,128)(2,1)} %bitcast.65, ...), custom_call_target="tpu_custom_call" | custom-call | flops 3000000000 | bytes 3094276 | tf_op jit(solution)/shard_map/fine_forward/pallas_call | solution.py:307
  18.7 2.2 %collective-permute-start.3 = (bf16[54,512]{1,0:T(8,128)(2,1)}, bf16[54,512]{1,0:T(8,128)(2,1)S(1)}, u32[]{:S(2)}, u32[]{:S(2)}) collective-permute-start(bf16[54,512]{1,0:T(8,128)(2,1)} %get-tuple-element.38), channel_id=1, source_target_pairs={{0,24},{1,25},{2,26},{3,27},{4,28},{5,29},{6,30},{7,31},{8,0},{9,1... | collective-permute-start | bytes 165896 | tf_op jit(solution)/shard_map/ppermute | solution.py:339
  20.9 2.5 %collective-permute-start.4 = (bf16[54,512]{1,0:T(8,128)(2,1)}, bf16[54,512]{1,0:T(8,128)(2,1)S(1)}, u32[]{:S(2)}, u32[]{:S(2)}) collective-permute-start(bf16[54,512]{1,0:T(8,128)(2,1)} %get-tuple-element.39), channel_id=1, source_target_pairs={{0,7},{1,0},{2,1},{3,2},{4,3},{5,4},{6,5},{7,6},{8,15},{9,8},{10,9... | collective-permute-start | bytes 165896 | tf_op jit(solution)/shard_map/ppermute | solution.py:339
  24.0 3.5 %collective-permute-done.6.refs_10_ = bf16[18,512]{1,0:T(8,128)(2,1)S(1)} collective-permute-done((bf16[18,512]{1,0:T(8,128)(2,1)S(1)}, bf16[18,512]{1,0:T(8,128)(2,1)S(1)}, u32[]{:S(2)}, u32[]{:S(2)}) %collective-permute-start.6) | collective-permute-done | bytes 18464 | tf_op jit(solution)/shard_map/ppermute | solution.py:339
  29.4 1.7 %collective-permute-done.5.refs_4_ = bf16[18,512]{1,0:T(8,128)(2,1)S(1)} collective-permute-done((bf16[18,512]{1,0:T(8,128)(2,1)}, bf16[18,512]{1,0:T(8,128)(2,1)S(1)}, u32[]{:S(2)}, u32[]{:S(2)}) %collective-permute-start.5) | collective-permute-done | bytes 18464 | tf_op jit(solution)/shard_map/ppermute | solution.py:339
  31.7 10.4 %coarse.1 = (bf16[72,512]{1,0:T(8,128)(2,1)}, bf16[288,512]{1,0:T(8,128)(2,1)}, bf16[54,512]{1,0:T(8,128)(2,1)}, bf16[54,512]{1,0:T(8,128)(2,1)}, bf16[18,512]{1...) custom-call(s32[1]{0:T(128)} %bitcast.refs_0_, ...), custom_call_target="tpu_custom_call" | custom-call | flops 8999999488 | bytes 9788900 | tf_op jit(solution)/shard_map/coarse/pallas_call | solution.py:307
  44.3 2.0 %collective-permute-start.12 = (bf16[54,512]{1,0:T(8,128)(2,1)}, bf16[54,512]{1,0:T(8,128)(2,1)S(1)}, u32[]{:S(2)}, u32[]{:S(2)}) collective-permute-start(bf16[54,512]{1,0:T(8,128)(2,1)} %get-tuple-element.43), channel_id=1, source_target_pairs={{0,8},{1,9},{2,10},{3,11},{4,12},{5,13},{6,14},{7,15},{8,16},{9,17... | collective-permute-start | bytes 165896 | tf_op jit(solution)/shard_map/ppermute | solution.py:339
  46.3 1.9 %collective-permute-start.13 = (bf16[54,512]{1,0:T(8,128)(2,1)}, bf16[54,512]{1,0:T(8,128)(2,1)S(1)}, u32[]{:S(2)}, u32[]{:S(2)}) collective-permute-start(bf16[54,512]{1,0:T(8,128)(2,1)} %get-tuple-element.44), channel_id=1, source_target_pairs={{0,1},{1,2},{2,3},{3,4},{4,5},{5,6},{6,7},{7,0},{8,9},{9,10},{10,1... | collective-permute-start | bytes 165896 | tf_op jit(solution)/shard_map/ppermute | solution.py:339
  48.2 1.5 %fusion.10 = (bf16[32,16,512]{2,1,0:T(8,128)(2,1)S(1)}, bf16[32,16,512]{2,1,0:T(8,128)(2,1)S(1)}, bf16[32,16,512]{2,1,0:T(8,128)(2,1)S(1)}) fusion(bf16[32,16,1536]{2,1,0:T(8,128)(2,1)} %bitcast.56), kind=kLoop, calls=%fused_computation.42 | loop fusion | bytes 3145728 | tf_op jit(solution)/shard_map/slice | solution.py:458
  53.9 1.6 %collective-permute-start.14 = (bf16[18,512]{1,0:T(8,128)(2,1)S(1)}, bf16[18,512]{1,0:T(8,128)(2,1)S(1)}, u32[]{:S(2)}, u32[]{:S(2)}) collective-permute-start(bf16[18,512]{1,0:T(8,128)(2,1)S(1)} %copy-done.19), channel_id=1, source_target_pairs={{0,9},{1,10},{2,11},{3,12},{4,13},{5,14},{6,15},{7,8},{8,17},{9,18... | collective-permute-start | bytes 55304 | tf_op jit(solution)/shard_map/ppermute | solution.py:339
  56.1 5.1 %collective-permute-done.14.refs_4_ = bf16[18,512]{1,0:T(8,128)(2,1)S(1)} collective-permute-done((bf16[18,512]{1,0:T(8,128)(2,1)S(1)}, bf16[18,512]{1,0:T(8,128)(2,1)S(1)}, u32[]{:S(2)}, u32[]{:S(2)}) %collective-permute-start.14) | collective-permute-done | bytes 18464 | tf_op jit(solution)/shard_map/ppermute | solution.py:339
  61.9 7.9 %fine_backward.1 = (bf16[288,512]{1,0:T(8,128)(2,1)}, bf16[54,512]{1,0:T(8,128)(2,1)}, bf16[54,512]{1,0:T(8,128)(2,1)}, bf16[18,512]{1,0:T(8,128)(2,1)}, f32[1,5...) custom-call(s32[1]{0:T(128)} %bitcast.1.refs_0_, bf16[288,512]{1,0:T(8,128)(2,1)} %get-tuple-element.42.refs_1_, ...), custom_call_target="tpu_custom_call" | custom-call | flops 6000000000 | bytes 4144900 | tf_op jit(solution)/shard_map/fine_backward/pallas_call | solution.py:307
  69.8 1.7 %slice_dynamic-update-slice_fusion.2 = bf16[32,112,256]{2,1,0:T(8,128)(2,1)} fusion(bf16[32,112,256]{2,1,0:T(8,128)(2,1)} %slice_dynamic-update-slice_fusion.3, bf16[32,16,768]{2,1,0:T(8,128)(2,1)} %bitcast.57), kind=kLoop, calls=%fused_computation.15 | loop fusion | bytes 524288
  71.5 1.7 %slice_dynamic-update-slice_fusion.1 = bf16[32,112,256]{2,1,0:T(8,128)(2,1)} fusion(bf16[32,112,256]{2,1,0:T(8,128)(2,1)} %slice_dynamic-update-slice_fusion.2, bf16[32,16,768]{2,1,0:T(8,128)(2,1)} %bitcast.58), kind=kLoop, calls=%fused_computation.14 | loop fusion | bytes 524288
  73.2 1.7 %slice_dynamic-update-slice_fusion = bf16[32,112,256]{2,1,0:T(8,128)(2,1)} fusion(bf16[32,112,256]{2,1,0:T(8,128)(2,1)} %slice_dynamic-update-slice_fusion.1, bf16[32,16,768]{2,1,0:T(8,128)(2,1)} %bitcast.59), kind=kLoop, calls=%fused_computation.13 | loop fusion | bytes 524288
  74.9 1.6 %slice_dynamic-update-slice_fusion.6 = bf16[32,112,256]{2,1,0:T(8,128)(2,1)} fusion(bf16[32,112,256]{2,1,0:T(8,128)(2,1)} %slice_dynamic-update-slice_fusion, bf16[32,8,512]{2,1,0:T(8,128)(2,1)} %bitcast.63), kind=kLoop, calls=%fused_computation.19 | loop fusion | bytes 262144
  78.1 1.8 %copy.58 = bf16[2,2,2,2,2,112,256]{6,5,4,3,2,1,0:T(8,128)(2,1)S(1)} copy(bf16[2,2,2,2,2,112,256]{6,5,0,2,3,1,4:T(8,128)(2,1)} %bitcast.18) | data formatting | bytes 3670016 | tf_op jit(solution)/shard_map/transpose | solution.py:436
  80.1 37.5 %gradient_sums.1 = (f32[1,64,512]{2,1,0:T(8,128)S(1)}, f32[1,48,512]{2,1,0:T(8,128)S(1)}, f32[1,112,256]{2,1,0:T(8,128)S(1)}) custom-call(bf16[32,64,512]{2,1,0:T(8,128)(2,1)S(1)} %bitcast.51, bf16[32,48,512]{2,1,0:T(8,128)(2,1)S(1)} %bitcast.53, bf16[32,112,256]{2,1,0:T(8,128)(2,1)S(1)} %bitcast.52), custom_call_target="tpu_custom_call" | custom-call | flops 10000000 | bytes 100000000 | tf_op jit(solution)/shard_map/gradient_sums/pallas_call | solution.py:439
  118.8 1.7 %collective-permute-start.17 = (bf16[18,512]{1,0:T(8,128)(2,1)S(1)}, bf16[18,512]{1,0:T(8,128)(2,1)S(1)}, u32[]{:S(2)}, u32[]{:S(2)}) collective-permute-start(bf16[18,512]{1,0:T(8,128)(2,1)S(1)} %copy-done.20), channel_id=1, source_target_pairs={{0,9},{1,10},{2,11},{3,12},{4,13},{5,14},{6,15},{7,8},{8,17},{9,18... | collective-permute-start | bytes 55304 | tf_op jit(solution)/shard_map/ppermute | solution.py:339
  123.7 2.4 %collective-permute-done.17.p2 = bf16[18,512]{1,0:T(8,128)(2,1)S(1)} collective-permute-done((bf16[18,512]{1,0:T(8,128)(2,1)S(1)}, bf16[18,512]{1,0:T(8,128)(2,1)S(1)}, u32[]{:S(2)}, u32[]{:S(2)}) %collective-permute-start.17) | collective-permute-done | bytes 18464 | tf_op jit(solution)/shard_map/ppermute | solution.py:339
  126.8 2.5 %final_roll.1 = bf16[288,512]{1,0:T(8,128)(2,1)} custom-call(bf16[288,512]{1,0:T(8,128)(2,1)} %get-tuple-element.49.own, bf16[54,512]{1,0:T(8,128)(2,1)} %copy-done.5, bf16[54,512]{1,0:T(8,128)(2,1)} %copy-done.6, bf16[18,512]{1,0:T(8,128)(2,1)} %copy-done.7, bf16[288,288]{1,0:T(8,128)(2,1)} %constant.107.clone.m0, bf16[288,54]{1,0:T(8,128)(2,1)} %constant.108.clone.m1, ...), custom_call_target="tpu_custom_call" | custom-call | flops 100000000 | bytes 957312 | tf_op jit(solution)/shard_map/final_roll/pallas_call | solution.py:307
  (114 shorter events, 21.6 us)
Async XLA Ops:
  1.6 11.8 %collective-permute-start = (bf16[54,512]{1,0:T(8,128)(2,1)S(1)}, bf16[54,512]{1,0:T(8,128)(2,1)S(1)}, u32[]{:S(2)}, u32[]{:S(2)}) collective-permute-start(bf16[54,512]{1,0:T(8,128)(2,1)S(1)} %reshape.164), channel_id=1, source_target_pairs={{0,24},{1,25},{2,26},{3,27},{4,28},{5,29},{6,30},{7,31},{8,0},{9,1... | collective-permute-start | bytes 165896 | tf_op jit(solution)/shard_map/ppermute | solution.py:339
  7.6 5.7 %collective-permute-start.1 = (bf16[54,512]{1,0:T(8,128)(2,1)S(1)}, bf16[54,512]{1,0:T(8,128)(2,1)S(1)}, u32[]{:S(2)}, u32[]{:S(2)}) collective-permute-start(bf16[54,512]{1,0:T(8,128)(2,1)S(1)} %reshape.165), channel_id=1, source_target_pairs={{0,7},{1,0},{2,1},{3,2},{4,3},{5,4},{6,5},{7,6},{8,15},{9,8},{10,9... | collective-permute-start | bytes 165896 | tf_op jit(solution)/shard_map/ppermute | solution.py:339
  10.0 3.3 %collective-permute-start.2 = (bf16[18,512]{1,0:T(8,128)(2,1)S(1)}, bf16[18,512]{1,0:T(8,128)(2,1)S(1)}, u32[]{:S(2)}, u32[]{:S(2)}) collective-permute-start(bf16[18,512]{1,0:T(8,128)(2,1)S(1)} %reshape.166), channel_id=1, source_target_pairs={{0,31},{1,24},{2,25},{3,26},{4,27},{5,28},{6,29},{7,30},{8,7},{9,0... | collective-permute-start | bytes 55304 | tf_op jit(solution)/shard_map/ppermute | solution.py:339
  14.0 9.4 %copy-start.3 = (bf16[6,12,512]{2,1,0:T(8,128)(2,1)S(1)}, bf16[6,12,512]{2,1,0:T(8,128)(2,1)}, u32[]{:S(2)}) copy-start(bf16[6,12,512]{2,1,0:T(8,128)(2,1)} %param.48) | copy-start | bytes 221188
  18.7 12.3 %collective-permute-start.3 = (bf16[54,512]{1,0:T(8,128)(2,1)}, bf16[54,512]{1,0:T(8,128)(2,1)S(1)}, u32[]{:S(2)}, u32[]{:S(2)}) collective-permute-start(bf16[54,512]{1,0:T(8,128)(2,1)} %get-tuple-element.38), channel_id=1, source_target_pairs={{0,24},{1,25},{2,26},{3,27},{4,28},{5,29},{6,30},{7,31},{8,0},{9,1... | collective-permute-start | bytes 165896 | tf_op jit(solution)/shard_map/ppermute | solution.py:339
  20.9 10.1 %collective-permute-start.4 = (bf16[54,512]{1,0:T(8,128)(2,1)}, bf16[54,512]{1,0:T(8,128)(2,1)S(1)}, u32[]{:S(2)}, u32[]{:S(2)}) collective-permute-start(bf16[54,512]{1,0:T(8,128)(2,1)} %get-tuple-element.39), channel_id=1, source_target_pairs={{0,7},{1,0},{2,1},{3,2},{4,3},{5,4},{6,5},{7,6},{8,15},{9,8},{10,9... | collective-permute-start | bytes 165896 | tf_op jit(solution)/shard_map/ppermute | solution.py:339
  23.4 4.1 %collective-permute-start.6 = (bf16[18,512]{1,0:T(8,128)(2,1)S(1)}, bf16[18,512]{1,0:T(8,128)(2,1)S(1)}, u32[]{:S(2)}, u32[]{:S(2)}) collective-permute-start(bf16[18,512]{1,0:T(8,128)(2,1)S(1)} %reshape.168), channel_id=1, source_target_pairs={{0,24},{1,25},{2,26},{3,27},{4,28},{5,29},{6,30},{7,31},{8,0},{9,1... | collective-permute-start | bytes 55304 | tf_op jit(solution)/shard_map/ppermute | solution.py:339
  23.9 5.5 %collective-permute-start.7 = (bf16[18,512]{1,0:T(8,128)(2,1)S(1)}, bf16[18,512]{1,0:T(8,128)(2,1)S(1)}, u32[]{:S(2)}, u32[]{:S(2)}) collective-permute-start(bf16[18,512]{1,0:T(8,128)(2,1)S(1)} %reshape.169), channel_id=1, source_target_pairs={{0,7},{1,0},{2,1},{3,2},{4,3},{5,4},{6,5},{7,6},{8,15},{9,8},{10,9... | collective-permute-start | bytes 55304 | tf_op jit(solution)/shard_map/ppermute | solution.py:339
  23.9 5.4 %collective-permute-start.8 = (bf16[18,512]{1,0:T(8,128)(2,1)S(1)}, bf16[18,512]{1,0:T(8,128)(2,1)S(1)}, u32[]{:S(2)}, u32[]{:S(2)}) collective-permute-start(bf16[18,512]{1,0:T(8,128)(2,1)S(1)} %reshape.170), channel_id=1, source_target_pairs={{0,31},{1,24},{2,25},{3,26},{4,27},{5,28},{6,29},{7,30},{8,7},{9,0... | collective-permute-start | bytes 55304 | tf_op jit(solution)/shard_map/ppermute | solution.py:339
  27.6 3.5 %collective-permute-start.5 = (bf16[18,512]{1,0:T(8,128)(2,1)}, bf16[18,512]{1,0:T(8,128)(2,1)S(1)}, u32[]{:S(2)}, u32[]{:S(2)}) collective-permute-start(bf16[18,512]{1,0:T(8,128)(2,1)} %get-tuple-element.40), channel_id=1, source_target_pairs={{0,31},{1,24},{2,25},{3,26},{4,27},{5,28},{6,29},{7,30},{8,7},{9,0... | collective-permute-start | bytes 55304 | tf_op jit(solution)/shard_map/ppermute | solution.py:339
  42.0 7.7 %copy-start.2 = (bf16[512,512]{1,0:T(8,128)(2,1)S(1)}, bf16[512,512]{1,0:T(8,128)(2,1)}, u32[]{:S(2)}) copy-start(bf16[512,512]{1,0:T(8,128)(2,1)} %get-tuple-element.55) | copy-start | bytes 1572868
  43.0 10.9 %collective-permute-start.11 = (bf16[3,6,512]{2,1,0:T(8,128)(2,1)S(1)}, bf16[3,6,512]{2,1,0:T(8,128)(2,1)S(1)}, u32[]{:S(2)}, u32[]{:S(2)}) collective-permute-start(bf16[3,6,512]{2,1,0:T(8,128)(2,1)S(1)} %get-tuple-element.81), channel_id=1, source_target_pairs={{0,1},{1,2},{2,3},{3,4},{4,5},{5,6},{6,7},{7,0},{8,9},{9,10},{10,1... | collective-permute-start | bytes 55304 | tf_op jit(solution)/shard_map/ppermute | solution.py:339
  43.1 12.4 %collective-permute-start.10 = (bf16[3,6,512]{2,1,0:T(8,128)(2,1)S(1)}, bf16[3,6,512]{2,1,0:T(8,128)(2,1)S(1)}, u32[]{:S(2)}, u32[]{:S(2)}) collective-permute-start(bf16[3,6,512]{2,1,0:T(8,128)(2,1)S(1)} %get-tuple-element.82), channel_id=1, source_target_pairs={{0,8},{1,9},{2,10},{3,11},{4,12},{5,13},{6,14},{7,15},{8,16},{9,17... | collective-permute-start | bytes 55304 | tf_op jit(solution)/shard_map/ppermute | solution.py:339
  43.1 12.3 %collective-permute-start.9 = (bf16[3,6,512]{2,1,0:T(8,128)(2,1)S(1)}, bf16[3,6,512]{2,1,0:T(8,128)(2,1)S(1)}, u32[]{:S(2)}, u32[]{:S(2)}) collective-permute-start(bf16[3,6,512]{2,1,0:T(8,128)(2,1)S(1)} %get-tuple-element.79), channel_id=1, source_target_pairs={{0,9},{1,10},{2,11},{3,12},{4,13},{5,14},{6,15},{7,8},{8,17},{9,18... | collective-permute-start | bytes 55304 | tf_op jit(solution)/shard_map/ppermute | solution.py:339
  44.3 16.9 %collective-permute-start.12 = (bf16[54,512]{1,0:T(8,128)(2,1)}, bf16[54,512]{1,0:T(8,128)(2,1)S(1)}, u32[]{:S(2)}, u32[]{:S(2)}) collective-permute-start(bf16[54,512]{1,0:T(8,128)(2,1)} %get-tuple-element.43), channel_id=1, source_target_pairs={{0,8},{1,9},{2,10},{3,11},{4,12},{5,13},{6,14},{7,15},{8,16},{9,17... | collective-permute-start | bytes 165896 | tf_op jit(solution)/shard_map/ppermute | solution.py:339
  46.3 14.9 %collective-permute-start.13 = (bf16[54,512]{1,0:T(8,128)(2,1)}, bf16[54,512]{1,0:T(8,128)(2,1)S(1)}, u32[]{:S(2)}, u32[]{:S(2)}) collective-permute-start(bf16[54,512]{1,0:T(8,128)(2,1)} %get-tuple-element.44), channel_id=1, source_target_pairs={{0,1},{1,2},{2,3},{3,4},{4,5},{5,6},{6,7},{7,0},{8,9},{9,10},{10,1... | collective-permute-start | bytes 165896 | tf_op jit(solution)/shard_map/ppermute | solution.py:339
  53.9 7.3 %collective-permute-start.14 = (bf16[18,512]{1,0:T(8,128)(2,1)S(1)}, bf16[18,512]{1,0:T(8,128)(2,1)S(1)}, u32[]{:S(2)}, u32[]{:S(2)}) collective-permute-start(bf16[18,512]{1,0:T(8,128)(2,1)S(1)} %copy-done.19), channel_id=1, source_target_pairs={{0,9},{1,10},{2,11},{3,12},{4,13},{5,14},{6,15},{7,8},{8,17},{9,18... | collective-permute-start | bytes 55304 | tf_op jit(solution)/shard_map/ppermute | solution.py:339
  69.7 7.4 %copy-start.10 = (f32[1,512]{1,0:T(1,128)S(1)}, f32[1,512]{1,0:T(1,128)}, u32[]{:S(2)}) copy-start(f32[1,512]{1,0:T(1,128)} %get-tuple-element.58) | copy-start | bytes 6148
  80.0 38.7 %copy-start.12 = (bf16[54,512]{1,0:T(8,128)(2,1)S(1)}, bf16[54,512]{1,0:T(8,128)(2,1)}, u32[]{:S(2)}) copy-start(bf16[54,512]{1,0:T(8,128)(2,1)} %get-tuple-element.50) | copy-start | bytes 165892
  80.1 38.7 %copy-start.11 = (bf16[54,512]{1,0:T(8,128)(2,1)S(1)}, bf16[54,512]{1,0:T(8,128)(2,1)}, u32[]{:S(2)}) copy-start(bf16[54,512]{1,0:T(8,128)(2,1)} %get-tuple-element.51) | copy-start | bytes 165892
  80.1 38.7 %copy-start.20 = (bf16[18,512]{1,0:T(8,128)(2,1)S(1)}, bf16[18,512]{1,0:T(8,128)(2,1)}, u32[]{:S(2)}) copy-start(bf16[18,512]{1,0:T(8,128)(2,1)} %get-tuple-element.52) | copy-start | bytes 55300
  118.7 7.4 %collective-permute-start.15 = (bf16[54,512]{1,0:T(8,128)(2,1)S(1)}, bf16[54,512]{1,0:T(8,128)(2,1)S(1)}, u32[]{:S(2)}, u32[]{:S(2)}) collective-permute-start(bf16[54,512]{1,0:T(8,128)(2,1)S(1)} %copy-done.12), channel_id=1, source_target_pairs={{0,8},{1,9},{2,10},{3,11},{4,12},{5,13},{6,14},{7,15},{8,16},{9,17... | collective-permute-start | bytes 165896 | tf_op jit(solution)/shard_map/ppermute | solution.py:339
  118.7 7.4 %collective-permute-start.16 = (bf16[54,512]{1,0:T(8,128)(2,1)S(1)}, bf16[54,512]{1,0:T(8,128)(2,1)S(1)}, u32[]{:S(2)}, u32[]{:S(2)}) collective-permute-start(bf16[54,512]{1,0:T(8,128)(2,1)S(1)} %copy-done.11), channel_id=1, source_target_pairs={{0,1},{1,2},{2,3},{3,4},{4,5},{5,6},{6,7},{7,0},{8,9},{9,10},{10,1... | collective-permute-start | bytes 165896 | tf_op jit(solution)/shard_map/ppermute | solution.py:339
  118.8 7.3 %collective-permute-start.17 = (bf16[18,512]{1,0:T(8,128)(2,1)S(1)}, bf16[18,512]{1,0:T(8,128)(2,1)S(1)}, u32[]{:S(2)}, u32[]{:S(2)}) collective-permute-start(bf16[18,512]{1,0:T(8,128)(2,1)S(1)} %copy-done.20), channel_id=1, source_target_pairs={{0,9},{1,10},{2,11},{3,12},{4,13},{5,14},{6,15},{7,8},{8,17},{9,18... | collective-permute-start | bytes 55304 | tf_op jit(solution)/shard_map/ppermute | solution.py:339
  (21 other events, 30.1 us)

commit v4 on v3

--- a/solution.py
+++ b/solution.py
@@ -316,6 +316,56 @@
     )(*operands)
 
 
+def exchange_kernel(moves, count, *refs):
+    sources, outs = refs[:count], refs[count : 2 * count]
+    send_sem, recv_sem = refs[2 * count :]
+    lats, lons = lax.axis_size("lat"), lax.axis_size("lon")
+    lat, lon = lax.axis_index("lat"), lax.axis_index("lon")
+
+    def at(lat_step, lon_step):
+        return ((lat + lat_step + lats) % lats, (lon + lon_step + lons) % lons)
+
+    barrier = pltpu.get_barrier_semaphore()
+    for a, b in moves:
+        pl.semaphore_signal(
+            barrier, inc=1, device_id=at(-a, -b), device_id_type=pl.DeviceIdType.MESH
+        )
+    pl.semaphore_wait(barrier, len(moves))
+    copies = []
+    for k in range(count):
+        copy = pltpu.make_async_remote_copy(
+            src_ref=sources[k],
+            dst_ref=outs[k],
+            send_sem=send_sem.at[k],
+            recv_sem=recv_sem.at[k],
+            device_id=at(*moves[k % len(moves)]),
+            device_id_type=pl.DeviceIdType.MESH,
+        )
+        copy.start()
+        copies.append(copy)
+    for copy in copies:
+        copy.wait()
+
+
+def exchange(parts, ahead, ident):
+    step = -1 if ahead else 1
+    moves = ((step, 0), (0, step), (step, step))
+    return list(
+        pl.pallas_call(
+            functools.partial(exchange_kernel, moves, len(parts)),
+            name=f"exchange_{ident}",
+            out_shape=[jax.ShapeDtypeStruct(v.shape, v.dtype) for v in parts],
+            in_specs=[VMEM] * len(parts),
+            out_specs=[VMEM] * len(parts),
+            scratch_shapes=[
+                pltpu.SemaphoreType.DMA((len(parts),)),
+                pltpu.SemaphoreType.DMA((len(parts),)),
+            ],
+            compiler_params=pltpu.CompilerParams(collective_id=ident, has_side_effects=True),
+        )(*parts)
+    )
+
+
 def cut_parts(grid, ahead):
     if ahead:
         lat, lon = (slice(None, SLAT), slice(SLAT, None)), (slice(None, SLON), slice(SLON, None))
@@ -497,8 +547,8 @@
     part_outs = [((n, breadth), BF16) for n in sizes]
     windowed, natural, merged = window_order(*fine), natural_order(*fine), merge_order(*fine)
 
-    arrived = send_parts(cut_parts(tokens, True), True)
-    cotangent_parts = send_parts(cut_parts(cotangent, True), True)
+    arrived = exchange(cut_parts(tokens, True) + cut_parts(cotangent, True), True, 1)
+    arrived, cotangent_parts = arrived[:3], arrived[3:]
     inner = fine_proj.shape[0]
     rolled_fine, packed, blend, result, *parts = call(
         functools.partial(fine_forward_kernel, fine_cols // WLON),
@@ -515,7 +565,7 @@
         True,
         3 * 10**9,
     )
-    arrived = send_parts(parts, True)
+    arrived = exchange(parts, True, 2)
     coarse_inner = coarse_proj.shape[0]
     coarse_windowed = window_order(*coarse)
     found = call(
@@ -540,7 +590,7 @@
     coarse_result, grad_grid = found[:2]
     merge_gain_sum, merge_weight_sum, coarse_gain_sum = found[5][0], found[6], found[7][0]
     coarse_qkv_sum, coarse_proj_sum = found[8:]
-    arrived = send_parts(found[2:5], False)
+    arrived = exchange(found[2:5], False, 3)
     grad_rolled, *parts = call(
         functools.partial(fine_backward_kernel, fine_cols // WLON),
         "fine_backward",

time: 130 us -> 128 us (0.985)
  Pallas kernels: 62.8 us -> 96.9 us
  starting transfers between devices: 22.6 us -> 2.3 us
  waiting for transfers between devices: 15.2 us -> 5.38 us
  local copies, waits for them, and re-layouts: 21.7 us -> 14.8 us
    pallas_call x0 -> x3, Pallas kernels: none -> 30.2 us  [exchange(): pl.pallas_call(functools.partial(exchange_kernel, moves, len(parts)), nam...]
    ppermute x18 -> x6, starting transfers between devices: 22.6 us -> 2.3 us  [send(): return lax.ppermute(value, ('lat', 'lon'), shift_pairs(lat_step, lon_step))]
    ppermute x18 -> x6, waiting for transfers between devices: 15.2 us -> 5.38 us  [send(): return lax.ppermute(value, ('lat', 'lon'), shift_pairs(lat_step, lon_step))]
    unnamed x61 -> x31, local copies, waits for them, and re-layouts: 12.3 us -> 4.38 us
    pallas_call x1, Pallas kernels: 37.5 us -> 41.2 us  [reduce_chunks(): pl.pallas_call(functools.partial(sum_kernel, orders), name='gradient_sums...]
    reshape x6, local copies, waits for them, and re-layouts: 0.1 us -> 3.75 us  [cut_parts(): return [grid[r, c].reshape(-1, grid.shape[2]) for r, c in picks]]
    transpose x2, local copies, waits for them, and re-layouts: 3.12 us -> 0.33 us  [reduce_chunks(): ready.append(moved.transpose(axes).reshape(chunk.shape))]
    slice x1, local copies, waits for them, and re-layouts: 1.5 us -> 0.19 us  [as_pieces(): parts = [value[:, :, i:i + width] for i in range(0, value.shape[2], width)]]
  transfers between devices with their start and end apart: 18 -> 6, of which waited for: 5 -> 1; matrix products, arithmetic and copies ran while one was open for 9% -> 7% of each run, Pallas kernels for 0% -> 32%
where the time goes in v4:
time: 128 us; the launch traced here: 127 us
  Pallas kernels  96.9 us (76%)
  local copies, waits for them, and re-layouts  14.8 us (12%)
  other arithmetic  6.77 us (5%)
  waiting for transfers between devices  5.38 us (4%)
  starting transfers between devices  2.3 us (2%)
    pallas_call x1, Pallas kernels, reduce_chunks(): pl.pallas_call(functools.partial(sum_kernel, orders), name='gradient_sums...  41.2 us
    pallas_call x3, Pallas kernels, exchange(): pl.pallas_call(functools.partial(exchange_kernel, moves, len(parts)), nam...  30.2 us
    pallas_call x4, Pallas kernels, call(): pl.pallas_call(body, name=name, out_shape=shapes, in_specs=[SMEM if scala...  25.5 us
    ppermute x6, waiting for transfers between devices, send(): return lax.ppermute(value, ('lat', 'lon'), shift_pairs(lat_step, lon_step))  5.38 us
    unnamed x31, local copies, waits for them, and re-layouts  4.38 us
    reshape x6, local copies, waits for them, and re-layouts, cut_parts(): return [grid[r, c].reshape(-1, grid.shape[2]) for r, c in picks]  3.75 us
    slice x4, local copies, waits for them, and re-layouts, cut_parts(): return [grid[r, c].reshape(-1, grid.shape[2]) for r, c in picks]  3.43 us
  transfers between devices with their start and end apart: 6, of which 1 were waited for; matrix products, arithmetic and copies ran while one was open for 7% of the time, Pallas kernels for 32%

profile of v4, /device:TPU:0, one launch (start us, length us, event | category | flops | bytes accessed | tf_op | source)
XLA Modules:
  0.0 127.1 jit_solution(10105774664148171958)
XLA Ops:
  0.6 0.9 slice.150
  1.6 0.9 slice.151
  2.4 0.7 slice.152
  3.2 0.9 fusion.12
  4.1 1.5 %reshape.170.refs_9_ = bf16[72,512]{1,0:T(8,128)(2,1)} reshape(bf16[6,12,512]{2,1,0:T(8,128)(2,1)} %param.48) | data formatting | bytes 147456 | tf_op jit(solution)/shard_map/reshape | solution.py:577
  7.5 0.6 reshape.164.refs_0_
  8.1 0.6 reshape.165.refs_1_
  9.4 10.6 %exchange_1.1 = (bf16[54,512]{1,0:T(8,128)(2,1)}, bf16[54,512]{1,0:T(8,128)(2,1)}, bf16[18,512]{1,0:T(8,128)(2,1)}, bf16[18,512]{1,0:T(8,128)(2,1)}, bf16[18,512]{1,0:T(8,128)(2,1)}, /*index=5*/bf16[18,512]{1,0:T(8,128)(2,1)}) custom-call(bf16[54,512]{1,0:T(8,128)(2,1)} %reshape.164.refs_0_, bf16[54,512]{1,0:T(8,128)(2,1)} %reshape.165.refs_1_, ...), custom_call_target="tpu_custom_call" | custom-call | tf_op jit(solution)/shard_map/exchange_1/pallas_call | solution.py:354
  20.0 4.7 %fine_forward.1 = (bf16[288,512]{1,0:T(8,128)(2,1)}, bf16[288,768]{1,0:T(8,128)(2,1)}, bf16[288,256]{1,0:T(8,128)(2,1)}, bf16[288,512]{1,0:T(8,128)(2,1)}, bf16[...) custom-call(s32[1]{0:T(128)} %bitcast.1.refs_0_, bf16[288,512]{1,0:T(8,128)(2,1)} %bitcast.66, ...), custom_call_target="tpu_custom_call" | custom-call | flops 3000000000 | bytes 3094276 | tf_op jit(solution)/shard_map/fine_forward/pallas_call | solution.py:307
  24.6 9.1 %exchange_2.1 = (bf16[54,512]{1,0:T(8,128)(2,1)}, bf16[54,512]{1,0:T(8,128)(2,1)}, bf16[18,512]{1,0:T(8,128)(2,1)}) custom-call(bf16[54,512]{1,0:T(8,128)(2,1)} %get-tuple-element.53.refs_0_, bf16[54,512]{1,0:T(8,128)(2,1)} %get-tuple-element.54.refs_1_, bf16[18,512]{1,0:T(8,128)(2,1)} %get-tuple-element.55.refs_2_), custom_call_target="tpu_custom_call" | custom-call | tf_op jit(solution)/shard_map/exchange_2/pallas_call | solution.py:354
  33.8 10.4 %coarse.1 = (bf16[72,512]{1,0:T(8,128)(2,1)}, bf16[288,512]{1,0:T(8,128)(2,1)}, bf16[54,512]{1,0:T(8,128)(2,1)}, bf16[54,512]{1,0:T(8,128)(2,1)}, bf16[18,512]{1...) custom-call(s32[1]{0:T(128)} %bitcast.refs_0_, ...), custom_call_target="tpu_custom_call" | custom-call | flops 8999999488 | bytes 9788900 | tf_op jit(solution)/shard_map/coarse/pallas_call | solution.py:307
  44.2 10.5 %exchange_3.1 = (bf16[54,512]{1,0:T(8,128)(2,1)}, bf16[54,512]{1,0:T(8,128)(2,1)}, bf16[18,512]{1,0:T(8,128)(2,1)}) custom-call(bf16[54,512]{1,0:T(8,128)(2,1)} %get-tuple-element.64.refs_0_, bf16[54,512]{1,0:T(8,128)(2,1)} %get-tuple-element.65.refs_1_, bf16[18,512]{1,0:T(8,128)(2,1)} %get-tuple-element.66.refs_2_), custom_call_target="tpu_custom_call" | custom-call | tf_op jit(solution)/shard_map/exchange_3/pallas_call | solution.py:354
  54.7 7.9 %fine_backward.1 = (bf16[288,512]{1,0:T(8,128)(2,1)}, bf16[54,512]{1,0:T(8,128)(2,1)}, bf16[54,512]{1,0:T(8,128)(2,1)}, bf16[18,512]{1,0:T(8,128)(2,1)}, f32[1,5...) custom-call(s32[1]{0:T(128)} %bitcast.1.refs_0_, bf16[288,512]{1,0:T(8,128)(2,1)} %get-tuple-element.63.refs_1_, ...), custom_call_target="tpu_custom_call" | custom-call | flops 6000000000 | bytes 4144900 | tf_op jit(solution)/shard_map/fine_backward/pallas_call | solution.py:307
  63.5 2.2 %collective-permute-start.1 = (bf16[3,6,512]{2,1,0:T(8,128)(2,1)}, bf16[3,6,512]{2,1,0:T(8,128)(2,1)}, u32[]{:S(2)}, u32[]{:S(2)}) collective-permute-start(bf16[3,6,512]{2,1,0:T(8,128)(2,1)} %get-tuple-element.106), channel_id=1, source_target_pairs={{0,8},{1,9},{2,10},{3,11},{4,12},{5,13},{6,14},{7,15},{8,16},{9,17... | collective-permute-start | bytes 55304 | tf_op jit(solution)/shard_map/ppermute | solution.py:389
  65.7 1.0 slice_dynamic-update-slice_fusion.2
  67.1 0.7 convert_reduce_fusion.1
  68.2 1.2 copy-done.1
  69.9 1.4 %copy-done = bf16[2048,512]{1,0:T(8,128)(2,1)S(1)} copy-done((bf16[2048,512]{1,0:T(8,128)(2,1)S(1)}, bf16[2048,512]{1,0:T(8,128)(2,1)}, u32[]{:S(2)}) %copy-start) | copy-done | bytes 2097176
  71.5 41.2 %gradient_sums.1 = (f32[1,64,512]{2,1,0:T(8,128)S(1)}, f32[1,48,512]{2,1,0:T(8,128)S(1)}, f32[1,112,256]{2,1,0:T(8,128)S(1)}) custom-call(bf16[32,64,512]{2,1,0:T(8,128)(2,1)S(1)} %bitcast.51, bf16[32,48,512]{2,1,0:T(8,128)(2,1)S(1)} %bitcast.53, bf16[32,112,256]{2,1,0:T(8,128)(2,1)S(1)} %bitcast.52), custom_call_target="tpu_custom_call" | custom-call | flops 10000000 | bytes 100000000 | tf_op jit(solution)/shard_map/gradient_sums/pallas_call | solution.py:489
  113.9 0.7 multiply_bitcast_fusion
  115.2 0.7 maximum_multiply_fusion
  117.2 1.5 %maximum_maximum_fusion = bf16[6,12,512]{2,1,0:T(8,128)(2,1)} fusion(bf16[3,6,512]{2,1,0:T(8,128)(2,1)S(1)} %get-tuple-element.104, bf16[3,6,512]{2,1,0:T(8,128)(2,1)} %collective-permute-done.2, bf16[3,6,512]{2,1,0:T(8,128)(2,1)} %collective-permute-done.1, bf16[3,6,512]{2,1,0:T(8,128)(2,1)} %collective-permute-done), kind=kLoop, calls=%fused_computation.21 | loop fusion | flops 294912 | bytes 147456 | tf_op jit(solution)/shard_map/concatenate | solution.py:397
  118.6 5.4 %collective-permute-done.5.p2 = bf16[18,512]{1,0:T(8,128)(2,1)S(1)} collective-permute-done((bf16[18,512]{1,0:T(8,128)(2,1)S(1)}, bf16[18,512]{1,0:T(8,128)(2,1)S(1)}, u32[]{:S(2)}, u32[]{:S(2)}) %collective-permute-start.5) | collective-permute-done | bytes 18464 | tf_op jit(solution)/shard_map/ppermute | solution.py:389
  124.6 2.5 %final_roll.1 = bf16[288,512]{1,0:T(8,128)(2,1)} custom-call(bf16[288,512]{1,0:T(8,128)(2,1)} %get-tuple-element.73.own, bf16[54,512]{1,0:T(8,128)(2,1)} %copy-done.6, bf16[54,512]{1,0:T(8,128)(2,1)} %copy-done.7, bf16[18,512]{1,0:T(8,128)(2,1)} %copy-done.8, bf16[288,288]{1,0:T(8,128)(2,1)} %constant.107.clone.m0, bf16[288,54]{1,0:T(8,128)(2,1)} %constant.108.clone.m1, ...), custom_call_target="tpu_custom_call" | custom-call | flops 100000000 | bytes 957312 | tf_op jit(solution)/shard_map/final_roll/pallas_call | solution.py:307
  (63 shorter events, 8.3 us)
Async XLA Ops:
  54.7 8.1 %copy-start.5 = (bf16[72,512]{1,0:T(8,128)(2,1)S(1)}, bf16[72,512]{1,0:T(8,128)(2,1)}, u32[]{:S(2)}) copy-start(bf16[72,512]{1,0:T(8,128)(2,1)} %get-tuple-element.62) | copy-start | bytes 221188
  54.7 11.0 %copy-start.3 = (bf16[512,512]{1,0:T(8,128)(2,1)S(1)}, bf16[512,512]{1,0:T(8,128)(2,1)}, u32[]{:S(2)}) copy-start(bf16[512,512]{1,0:T(8,128)(2,1)} %get-tuple-element.79) | copy-start | bytes 1572868
  62.6 4.1 %copy-start.2 = (bf16[512,768]{1,0:T(8,128)(2,1)S(1)}, bf16[512,768]{1,0:T(8,128)(2,1)}, u32[]{:S(2)}) copy-start(bf16[512,768]{1,0:T(8,128)(2,1)} %get-tuple-element.80) | copy-start | bytes 2359300
  62.7 4.1 %copy-start.4 = (bf16[256,512]{1,0:T(8,128)(2,1)S(1)}, bf16[256,512]{1,0:T(8,128)(2,1)}, u32[]{:S(2)}) copy-start(bf16[256,512]{1,0:T(8,128)(2,1)} %get-tuple-element.81) | copy-start | bytes 786436
  62.7 4.3 %copy-start.9 = (f32[1,2048]{1,0:T(1,128)S(1)}, f32[1,2048]{1,0:T(1,128)}, u32[]{:S(2)}) copy-start(f32[1,2048]{1,0:T(1,128)} %get-tuple-element.83) | copy-start | bytes 24580
  62.7 61.3 %collective-permute-start.3 = (bf16[54,512]{1,0:T(8,128)(2,1)}, bf16[54,512]{1,0:T(8,128)(2,1)S(1)}, u32[]{:S(2)}, u32[]{:S(2)}) collective-permute-start(bf16[54,512]{1,0:T(8,128)(2,1)} %get-tuple-element.74), channel_id=1, source_target_pairs={{0,8},{1,9},{2,10},{3,11},{4,12},{5,13},{6,14},{7,15},{8,16},{9,17... | collective-permute-start | bytes 165896 | tf_op jit(solution)/shard_map/ppermute | solution.py:389
  62.7 61.2 %collective-permute-start.4 = (bf16[54,512]{1,0:T(8,128)(2,1)}, bf16[54,512]{1,0:T(8,128)(2,1)S(1)}, u32[]{:S(2)}, u32[]{:S(2)}) collective-permute-start(bf16[54,512]{1,0:T(8,128)(2,1)} %get-tuple-element.75), channel_id=1, source_target_pairs={{0,1},{1,2},{2,3},{3,4},{4,5},{5,6},{6,7},{7,0},{8,9},{9,10},{10,1... | collective-permute-start | bytes 165896 | tf_op jit(solution)/shard_map/ppermute | solution.py:389
  62.8 4.0 %copy-start.10 = (f32[1,512]{1,0:T(1,128)S(1)}, f32[1,512]{1,0:T(1,128)}, u32[]{:S(2)}) copy-start(f32[1,512]{1,0:T(1,128)} %get-tuple-element.82) | copy-start | bytes 6148
  63.5 53.6 %collective-permute-start = (bf16[3,6,512]{2,1,0:T(8,128)(2,1)}, bf16[3,6,512]{2,1,0:T(8,128)(2,1)}, u32[]{:S(2)}, u32[]{:S(2)}) collective-permute-start(bf16[3,6,512]{2,1,0:T(8,128)(2,1)} %get-tuple-element.103), channel_id=1, source_target_pairs={{0,9},{1,10},{2,11},{3,12},{4,13},{5,14},{6,15},{7,8},{8,17},{9,18... | collective-permute-start | bytes 55304 | tf_op jit(solution)/shard_map/ppermute | solution.py:389
  63.5 53.6 %collective-permute-start.1 = (bf16[3,6,512]{2,1,0:T(8,128)(2,1)}, bf16[3,6,512]{2,1,0:T(8,128)(2,1)}, u32[]{:S(2)}, u32[]{:S(2)}) collective-permute-start(bf16[3,6,512]{2,1,0:T(8,128)(2,1)} %get-tuple-element.106), channel_id=1, source_target_pairs={{0,8},{1,9},{2,10},{3,11},{4,12},{5,13},{6,14},{7,15},{8,16},{9,17... | collective-permute-start | bytes 55304 | tf_op jit(solution)/shard_map/ppermute | solution.py:389
  65.7 51.5 %collective-permute-start.2 = (bf16[3,6,512]{2,1,0:T(8,128)(2,1)}, bf16[3,6,512]{2,1,0:T(8,128)(2,1)}, u32[]{:S(2)}, u32[]{:S(2)}) collective-permute-start(bf16[3,6,512]{2,1,0:T(8,128)(2,1)} %get-tuple-element.105), channel_id=1, source_target_pairs={{0,1},{1,2},{2,3},{3,4},{4,5},{5,6},{6,7},{7,0},{8,9},{9,10},{10,1... | collective-permute-start | bytes 55304 | tf_op jit(solution)/shard_map/ppermute | solution.py:389
  68.0 1.4 %copy-start.1 = (bf16[512,1536]{1,0:T(8,128)(2,1)S(1)}, bf16[512,1536]{1,0:T(8,128)(2,1)}, u32[]{:S(2)}) copy-start(bf16[512,1536]{1,0:T(8,128)(2,1)} %get-tuple-element.78) | copy-start | bytes 4718596
  69.7 1.6 %copy-start = (bf16[2048,512]{1,0:T(8,128)(2,1)S(1)}, bf16[2048,512]{1,0:T(8,128)(2,1)}, u32[]{:S(2)}) copy-start(bf16[2048,512]{1,0:T(8,128)(2,1)} %get-tuple-element.77) | copy-start | bytes 6291460
  71.5 45.6 %copy-start.11 = (bf16[18,512]{1,0:T(8,128)(2,1)S(1)}, bf16[18,512]{1,0:T(8,128)(2,1)}, u32[]{:S(2)}) copy-start(bf16[18,512]{1,0:T(8,128)(2,1)} %get-tuple-element.76) | copy-start | bytes 55300
  117.1 6.8 %collective-permute-start.5 = (bf16[18,512]{1,0:T(8,128)(2,1)S(1)}, bf16[18,512]{1,0:T(8,128)(2,1)S(1)}, u32[]{:S(2)}, u32[]{:S(2)}) collective-permute-start(bf16[18,512]{1,0:T(8,128)(2,1)S(1)} %copy-done.11), channel_id=1, source_target_pairs={{0,9},{1,10},{2,11},{3,12},{4,13},{5,14},{6,15},{7,8},{8,17},{9,18... | collective-permute-start | bytes 55304 | tf_op jit(solution)/shard_map/ppermute | solution.py:389
  124.0 0.6 copy-start.8
  124.0 0.6 copy-start.6
  124.0 0.6 copy-start.7
